TPU v7x, 128 devices: a whole 4x4x4 slice. The times are simulated.
128 devices in a mesh: row: 16 (over y_lo, z, core), col: 8 (over x, y_hi).
Axes of the slice: x: 4, y: 4 (y_hi: 2, y_lo: 2; y = y_hi * 2 + y_lo), z: 4, core: 2. Of those that a mesh axis runs over, the one named last changes fastest.
Arguments:
- potential: float32 [512, 512, 512], P(('row', 'col')), may hold values from -6 to 6
- basis_left: bfloat16 [8192, 128, 384], P(('row', 'col')), may hold values from -1.1953125 to 1.1953125
- basis_right: bfloat16 [8192, 128, 384], P(('row', 'col')), may hold values from -1.1953125 to 1.1953125
- core_matrix: bfloat16 [8192, 8192], P('row', 'col'), may hold values from -3 to 3
- density: bfloat16 [8192, 8192], P('row', 'col'), as said below
- pattern: int32 [64, 64], replicated, may hold values from 0 to 1, as said below
- pair_atoms: int32 [8192, 2], P(('row', 'col')), may hold values from 0 to 63, as said below
- cube_offsets: int32 [8192, 3], P(('row', 'col')), may hold values from 0 to 504, as said below
- live_count: int32 [128], P(('row', 'col')), may hold values from 32 to 64, as said below
Outputs:
- hamiltonian: bfloat16 [8192, 8192], P('row', 'col')
- product: float32 [8192, 8192], P('row', 'col')
Inputs may be any that keep to these rules, and one draw needn't show every extreme that they name: `pattern`: symmetric; every diagonal block is 1. density is symmetric. `pair_atoms`: the owner of block (i, j) is (i // 4, j // 8) on a 16 x 8 grid. Among the 64 entry slots of one slab at most 1 name blocks of one owner, and in every draw one owner is named by a live entry of every slab. `cube_offsets`: column 0 is at most 2, column 1 at most 504, column 2 at most 504. `live_count`: some slab uses all its slots.
All inputs are finite; a program needn't handle non-finite values.
Results may differ from a plain program's by a relative error of at most 0.0092.
Values may be sent and summed in bfloat16 or wider, within the bound.
A program may use at most 192 MiB of HBM per device.

v0:
```python
import functools

import jax
import jax.numpy as jnp
from jax import lax
from jax.sharding import Mesh
from jax.sharding import PartitionSpec as P

NATOMS = 64
HALO = 2
CUBE_X = 6
CUBE = 8
ROW = ("row_0", "row_1", "row_2")
ROW_COL = ("row_0", "row_1", "row_2", "col")


HIGHEST = lax.Precision.HIGHEST


def extended(array, sides, width):
    edges = {}
    for axis, dim in sides:
        size, length = (lax.axis_size(axis), array.shape[dim])
        up = [(i, (i + 1) % size) for i in range(size)]
        last = lax.slice_in_dim(array, length - width, length, axis=dim)
        leading = lax.slice_in_dim(array, 0, width, axis=dim)
        edges[dim] = (
            lax.ppermute(last, axis, up),
            lax.ppermute(leading, axis, [(b, a) for a, b in up]),
        )
    done = []
    for _, dim in sides:
        low, high = edges[dim]
        around = [(width, width) if d in done else (0, 0) for d in range(array.ndim)]
        array = jnp.concatenate([jnp.pad(low, around), array, jnp.pad(high, around)], axis=dim)
        done.append(dim)
    return array


def laid_out(pieces, dim):
    shape = list(pieces.shape[1:])
    shape[dim] *= pieces.shape[0]
    return jnp.moveaxis(pieces, 0, dim).reshape(shape)


def stacked_from(array, axes, sequence):
    pieces = array
    for k in sequence:
        pieces = lax.all_gather(pieces, axes[k])
    done = sequence[::-1]
    back = [done.index(k) for k in range(len(axes))]
    pieces = pieces.transpose(*back, *range(len(axes), pieces.ndim))
    return pieces.reshape(-1, *array.shape)


def gather_axes(array, axes, sequence, dim):
    return laid_out(stacked_from(array, axes, sequence), dim)


def block_mask(values, pattern_tile, block_size):
    row_blocks, col_blocks = pattern_tile.shape
    shaped = values.reshape(row_blocks, block_size, col_blocks, block_size)
    selected = (pattern_tile > 0)[:, None, :, None]
    kept = jnp.where(selected, shaped, jnp.zeros((), values.dtype))
    return kept.reshape(row_blocks * block_size, col_blocks * block_size)


def cut_cube(padded, offsets):
    corner = (offsets[0], offsets[1], offsets[2])
    return lax.dynamic_slice(padded, corner, (CUBE_X, CUBE, CUBE)).reshape(-1)


def shards(
    potential,
    basis_left,
    basis_right,
    core_matrix,
    density,
    pattern,
    pair_atoms,
    cube_offsets,
    live_count,
):
    row_count = lax.axis_size(ROW)
    col_count = lax.axis_size("col")
    devices = row_count * col_count
    block_size = basis_left.shape[1]
    entries = pair_atoms.shape[0]
    atom_rows = NATOMS // row_count
    atom_cols = NATOMS // col_count
    capacity = (entries + devices - 1) // devices
    slot_total = devices * capacity
    padded = extended(potential.astype(jnp.bfloat16), ((ROW_COL, 0),), HALO).astype(potential.dtype)
    potential_cubes = jax.vmap(functools.partial(cut_cube, padded))(cube_offsets)
    ordinal = jnp.arange(entries, dtype=jnp.int32)
    live_flag = (ordinal < live_count[0]).astype(jnp.float32)
    weighted = (basis_left * potential_cubes[:, None, :]).astype(jnp.bfloat16)
    partial_blocks = jnp.einsum(
        "eak,ebk->eab", weighted, basis_right, preferred_element_type=jnp.float32
    )
    partial_blocks = partial_blocks * live_flag[:, None, None]
    first_atom = pair_atoms[:, 0]
    second_atom = pair_atoms[:, 1]
    owner_index = first_atom // atom_rows * col_count + second_atom // atom_cols
    local_block = first_atom % atom_rows * atom_cols + second_atom % atom_cols
    earlier = (owner_index[:, None] == owner_index[None, :]) & (ordinal[None, :] < ordinal[:, None])
    placed = owner_index * capacity + jnp.sum(earlier.astype(jnp.int32), axis=1)
    sending = placed[None, :] == jnp.arange(slot_total, dtype=jnp.int32)[:, None]
    outgoing = jnp.dot(
        sending.astype(jnp.float32),
        partial_blocks.reshape(entries, block_size * block_size),
        precision=HIGHEST,
    )
    outgoing_ids = jnp.sum(jnp.where(sending, local_block[None, :], 0), axis=1)
    received, received_ids = (
        lax.all_to_all(
            outgoing.reshape(devices, capacity, block_size * block_size).astype(jnp.bfloat16),
            ROW_COL,
            split_axis=0,
            concat_axis=0,
            tiled=True,
        ).astype(jnp.float32),
        lax.all_to_all(
            outgoing_ids.reshape(devices, capacity),
            ROW_COL,
            split_axis=0,
            concat_axis=0,
            tiled=True,
        ),
    )
    received = received.reshape(slot_total, block_size * block_size)
    received_ids = received_ids.reshape(slot_total)
    gathering = (
        received_ids[None, :] == jnp.arange(atom_rows * atom_cols, dtype=jnp.int32)[:, None]
    ).astype(jnp.float32)
    integrals = jnp.dot(gathering, received, precision=HIGHEST)
    integrals = integrals.reshape(atom_rows, atom_cols, block_size, block_size).transpose(
        0, 2, 1, 3
    )
    integrals = integrals.reshape(atom_rows * block_size, atom_cols * block_size)
    corner = (lax.axis_index(ROW) * atom_rows, lax.axis_index("col") * atom_cols)
    pattern_tile = lax.dynamic_slice(pattern, corner, (atom_rows, atom_cols))
    hamiltonian = block_mask(
        core_matrix.astype(jnp.float32) + integrals, pattern_tile, block_size
    ).astype(jnp.bfloat16)
    masked_density = block_mask(density, pattern_tile, block_size)
    full_rows = lax.all_gather(hamiltonian, "col", axis=1, tiled=True)
    product = jnp.dot(
        full_rows,
        gather_axes(masked_density, ROW, (0, 1, 2), 0),
        preferred_element_type=jnp.float32,
    )
    return (hamiltonian, product)


def solution(mesh):
    split = Mesh(
        mesh.devices.reshape(2, 4, 2, mesh.shape["col"]), ("row_0", "row_1", "row_2", "col")
    )
    placed = (
        P(ROW_COL, None, None),
        P(ROW_COL, None, None),
        P(ROW_COL, None, None),
        P(ROW, "col"),
        P(ROW, "col"),
        P(),
        P(ROW_COL, None),
        P(ROW_COL, None),
        P(ROW_COL),
    )
    return jax.shard_map(
        shards,
        mesh=split,
        in_specs=placed,
        out_specs=(P(ROW, "col"), P(ROW, "col")),
        check_vma=False,
    )
```

profile of v0, /device:TPU:1, one launch (start us, length us, event | category | flops | bytes accessed | tf_op | source)
XLA Modules:
  0.0 629.1 jit_solution(15038382934699926828)
XLA Ops:
  10.7 38.8 %all-gather.10.cloned.1.call-done = bf16[1024,1024]{1,0:T(8,128)(2,1)} async-done(((bf16[512,1024]{1,0:T(8,128)(2,1)}), bf16[1024,1024]{1,0:T(8,128)(2,1)}) %all-gather.10.cloned.1.call-update) | async-done | bytes 2097168 | tf_op jit(solution)/shard_map/all_gather | solution.py:49
  55.9 2.9 collective-permute-start.1
  59.9 7.6 %all-to-all-start = ((s32[128,1,1]{2,1,0:T(1,128)}), s32[128,1,1]{2,1,0:T(1,128)S(1)}, u32[]{:S(2)}, u32[]{:S(2)}) async-start(s32[128,1,1]{2,1,0:T(1,128)} %copy.31), calls=%async_computation | async-start | bytes 131072 | tf_op jit(solution)/shard_map/all_to_all | solution.py:123
  68.4 32.5 %collective-permute-done = bf16[2,512,512]{2,1,0:T(8,128)(2,1)} collective-permute-done((bf16[2,512,512]{2,1,0:T(8,128)(2,1)}, bf16[2,512,512]{2,1,0:T(8,128)(2,1)}, u32[]{:S(2)}, u32[]{:S(2)}) %collective-permute-start) | collective-permute-done | bytes 1048608 | tf_op jit(solution)/shard_map/ppermute | solution.py:28
  100.9 4.7 collective-permute-done.1
  105.6 4.8 maximum_convert_fusion
  110.4 34.7 %all-gather.12.cloned.1.call-done = bf16[8,512,1024]{2,1,0:T(8,128)(2,1)} async-done(((bf16[2,512,1024]{2,1,0:T(8,128)(2,1)}), bf16[8,512,1024]{2,1,0:T(8,128)(2,1)}) %all-gather.12.cloned.1.call-update) | async-done | bytes 8388624 | tf_op jit(solution)/shard_map/all_gather | solution.py:49
  146.6 219.7 %while.1 = (s32[]{:T(128)}, f32[8,512,512]{2,1,0:T(8,128)}, s32[64,3]{0,1:T(4,128)S(1)}, f32[64,6,8,8]{3,2,1,0:T(8,128)S(1)}, s32[]{:T(128)}) while((s32[]{:T(128)}, f32[8,512,512]{2,1,0:T(8,128)}, s32[64,3]{0,1:T(4,128)S(1)}, f32[64,6,8,8]{3,2,1,0:T(8,128)S(1)}, s32[]{:T(128)}) %tuple.39), condition=%wide.while_cond, body=%wide.while_body.sunk | while | flops 2 | bytes 26249 | solution.py:70
  147.2 2.9 bitcast_dynamic-update-slice_fusion.2
  157.3 2.9 bitcast_dynamic-update-slice_fusion.2
  160.9 2.9 bitcast_dynamic-update-slice_fusion.2
  164.4 2.9 bitcast_dynamic-update-slice_fusion.2
  167.9 2.9 bitcast_dynamic-update-slice_fusion.2
  171.4 2.9 bitcast_dynamic-update-slice_fusion.2
  174.8 2.9 bitcast_dynamic-update-slice_fusion.2
  185.0 2.9 bitcast_dynamic-update-slice_fusion.2
  188.5 2.9 bitcast_dynamic-update-slice_fusion.2
  191.9 2.9 bitcast_dynamic-update-slice_fusion.2
  198.7 2.9 bitcast_dynamic-update-slice_fusion.2
  202.2 2.9 bitcast_dynamic-update-slice_fusion.2
  205.6 2.9 bitcast_dynamic-update-slice_fusion.2
  212.5 2.9 bitcast_dynamic-update-slice_fusion.2
  215.9 2.9 bitcast_dynamic-update-slice_fusion.2
  219.4 2.9 bitcast_dynamic-update-slice_fusion.2
  222.8 2.9 bitcast_dynamic-update-slice_fusion.2
  229.6 2.9 bitcast_dynamic-update-slice_fusion.2
  236.4 2.9 bitcast_dynamic-update-slice_fusion.2
  239.9 2.9 bitcast_dynamic-update-slice_fusion.2
  304.9 2.9 bitcast_dynamic-update-slice_fusion.2
  318.7 2.9 bitcast_dynamic-update-slice_fusion.2
  322.1 2.9 bitcast_dynamic-update-slice_fusion.2
  325.6 2.9 bitcast_dynamic-update-slice_fusion.2
  335.8 2.9 bitcast_dynamic-update-slice_fusion.2
  339.3 2.9 bitcast_dynamic-update-slice_fusion.2
  342.7 2.9 bitcast_dynamic-update-slice_fusion.2
  356.5 2.9 bitcast_dynamic-update-slice_fusion.2
  366.9 7.3 %broadcast_multiply_fusion = f32[64,128,128]{2,1,0:T(8,128)S(1)} fusion(f32[64]{0:T(128)S(1)} %compare_convert_fusion, bf16[64,128,384]{2,1,0:T(8,128)(2,1)} %param.11, bf16[64,128,384]{2,1,0:T(8,128)(2,1)} %param.10, f32[64,384]{1,0:T(8,128)S(1)} %copy.33), kind=kOutput, calls=%fused_computation.13 | convolution fusion | flops 815792128 | bytes 16875776 | tf_op jit(solution)/shard_map/eak,ebk->eab/dot_general | solution.py:98
  374.2 8.8 %fusion = bf16[128,1,16384]{2,0,1:T(8,128)(2,1)} fusion(f32[8,8,128,128]{3,2,1,0:T(8,128)S(1)} %bitcast.96, s32[64]{0:T(128)S(1)} %add.100), kind=kOutput, calls=%fused_computation.3 | convolution fusion | flops 1612718080 | bytes 8388864 | tf_op jit(solution)/shard_map/dot_general | solution.py:109
  383.5 6.7 %reduce.1 = bf16[128,16384]{1,0:T(8,128)(2,1)} reduce(bf16[128,1,16384]{2,0,1:T(8,128)(2,1)} %fusion, bf16[]{:T(256)} %broadcast.275), dimensions={1}, to_apply=%copy.34.reduce_sub_computation | reduce | bytes 8388610 | tf_op jit(solution)/shard_map/convert_element_type | solution.py:117
  390.2 7.8 %reshape.214 = bf16[128,2,8192]{2,1,0:T(2,128)(2,1)} reshape(bf16[128,16384]{1,0:T(8,128)(2,1)} %reduce.1) | data formatting | bytes 8388608
  398.0 9.6 %all-to-all-start.1 = ((bf16[128,2,8192]{2,1,0:T(2,128)(2,1)}), bf16[128,2,8192]{2,1,0:T(2,128)(2,1)}, u32[]{:S(2)}, u32[]{:S(2)}) async-start(bf16[128,2,8192]{2,1,0:T(2,128)(2,1)} %reshape.214), calls=%async_computation.1 | async-start | bytes 8388608 | tf_op jit(solution)/shard_map/all_to_all | solution.py:116
  410.2 48.6 %all-to-all-done.1 = bf16[128,2,8192]{2,1,0:T(2,128)(2,1)} async-done(((bf16[128,2,8192]{2,1,0:T(2,128)(2,1)}), bf16[128,2,8192]{2,1,0:T(2,128)(2,1)}, u32[]{:S(2)}, u32[]{:S(2)}) %all-to-all-start.1) | async-done | bytes 4194336 | tf_op jit(solution)/shard_map/all_to_all | solution.py:116
  458.8 19.8 %reshape.215 = bf16[128,1,16384]{2,1,0:T(2,128)(2,1)} reshape(bf16[128,2,8192]{2,1,0:T(2,128)(2,1)} %all-to-all-done.1) | data formatting | bytes 8388608
  478.6 17.2 %copy.39 = bf16[128,1,16384]{0,2,1:T(8,128)(2,1)} copy(bf16[128,1,16384]{2,1,0:T(2,128)(2,1)} %reshape.215) | data formatting | bytes 8388608 | tf_op jit(solution)/shard_map/dot_general | solution.py:136
  495.7 3.8 fusion.9
  501.4 14.0 %copy.36 = bf16[2,4,2,512,1024]{4,3,2,1,0:T(8,128)(2,1)} copy(bf16[2,4,2,512,1024]{4,3,0,1,2:T(8,128)(2,1)} %bitcast.98) | data formatting | bytes 33554432 | tf_op jit(solution)/shard_map/transpose | solution.py:52
  515.4 91.5 %all-gather.8.cloned.1.call-done = bf16[512,8192]{1,0:T(8,128)(2,1)} async-done(((bf16[512,1024]{1,0:T(8,128)(2,1)}), bf16[512,8192]{1,0:T(8,128)(2,1)}) %all-gather.8.cloned.1.call-update) | async-done | bytes 8388624 | tf_op jit(solution)/shard_map/all_gather | solution.py:147
  606.9 15.7 %fusion.18 = f32[512,1024]{1,0:T(8,128)} fusion(bf16[512,8192]{1,0:T(8,128)(2,1)} %all-gather.8.cloned.1.call-done, bf16[8192,1024]{1,0:T(8,128)(2,1)} %bitcast.99), kind=kOutput, calls=%fused_computation.59 | convolution fusion | flops 8589934592 | bytes 27262976 | tf_op jit(solution)/shard_map/dot_general | solution.py:148
  (204 shorter events, 157.8 us)
Async XLA Ops:
  7.2 42.3 %all-gather.10.cloned.1.call-start = ((), (), s32[]{:S(2)}) async-start(), calls=%async_computation.3 | async-start | bytes 3145728 | tf_op jit(solution)/shard_map/all_gather | solution.py:49
  10.7 134.4 %all-gather.12.cloned.1.call-start = ((), (), s32[]{:S(2)}) async-start(), calls=%async_computation.4 | async-start | bytes 10485760 | tf_op jit(solution)/shard_map/all_gather | solution.py:49
  49.5 9.3 %copy-start.3 = (s32[64,2]{0,1:T(2,128)S(1)}, s32[64,2]{0,1:T(2,128)}, u32[]{:S(2)}) copy-start(s32[64,2]{0,1:T(2,128)} %param.15) | copy-start | bytes 1540
  49.5 18.9 %copy-start.2 = (s32[64,3]{0,1:T(4,128)S(1)}, s32[64,3]{0,1:T(4,128)}, u32[]{:S(2)}) copy-start(s32[64,3]{0,1:T(4,128)} %param.16) | copy-start | bytes 2308
  53.5 47.5 %collective-permute-start = (bf16[2,512,512]{2,1,0:T(8,128)(2,1)}, bf16[2,512,512]{2,1,0:T(8,128)(2,1)}, u32[]{:S(2)}, u32[]{:S(2)}) collective-permute-start(bf16[2,512,512]{2,1,0:T(8,128)(2,1)} %get-tuple-element.21), channel_id=1, source_target_pairs={{0,1},{1,2},{2,3},{3,4},{4,5},{5,6},{6,7},{7,8},{8,9},{9,10},{10,1... | collective-permute-start | bytes 3145736 | tf_op jit(solution)/shard_map/ppermute | solution.py:28
  55.9 49.7 %collective-permute-start.1 = (bf16[2,512,512]{2,1,0:T(8,128)(2,1)}, bf16[2,512,512]{2,1,0:T(8,128)(2,1)}, u32[]{:S(2)}, u32[]{:S(2)}) collective-permute-start(bf16[2,512,512]{2,1,0:T(8,128)(2,1)} %get-tuple-element.22), channel_id=1, source_target_pairs={{1,0},{2,1},{3,2},{4,3},{5,4},{6,5},{7,6},{8,7},{9,8},{10,9},{11,1... | collective-permute-start | bytes 3145736 | tf_op jit(solution)/shard_map/ppermute | solution.py:29
  59.9 338.1 %all-to-all-start = ((s32[128,1,1]{2,1,0:T(1,128)}), s32[128,1,1]{2,1,0:T(1,128)S(1)}, u32[]{:S(2)}, u32[]{:S(2)}) async-start(s32[128,1,1]{2,1,0:T(1,128)} %copy.31), calls=%async_computation | async-start | bytes 131072 | tf_op jit(solution)/shard_map/all_to_all | solution.py:123
  67.5 433.8 %all-gather.14.cloned.1.call-start = ((), (), s32[]{:S(2)}) async-start(), calls=%async_computation.5 | async-start | bytes 25165824 | tf_op jit(solution)/shard_map/all_gather | solution.py:49
  145.1 1.4 copy-start
  398.0 60.8 %all-to-all-start.1 = ((bf16[128,2,8192]{2,1,0:T(2,128)(2,1)}), bf16[128,2,8192]{2,1,0:T(2,128)(2,1)}, u32[]{:S(2)}, u32[]{:S(2)}) async-start(bf16[128,2,8192]{2,1,0:T(2,128)(2,1)} %reshape.214), calls=%async_computation.1 | async-start | bytes 8388608 | tf_op jit(solution)/shard_map/all_to_all | solution.py:116
  407.6 199.3 %all-gather.8.cloned.1.call-start = ((), (), s32[]{:S(2)}) async-start(), calls=%async_computation.2 | async-start | bytes 9437184 | tf_op jit(solution)/shard_map/all_gather | solution.py:147
  495.7 3.8 copy-start.1
Sparse Core Ops, SparseCore 0:
  10.8 38.6 all-gather.9
  51.2 93.9 all-gather.11
  146.8 33.8 all-gather.13
  501.4 105.3 all-gather.7
where the time goes:
time: 635 us; the launch traced here: 629 us
  local copies, waits for them, and re-layouts  283 us (45%)
  waiting for transfers between devices  251 us (40%)
  matrix products  35.6 us (6%)
  starting transfers between devices  23.1 us (4%)
  other arithmetic  21.7 us (3%)
  between operations  14.6 us (2%)
    gather x192, local copies, waits for them, and re-layouts  220 us
    all_gather x1, waiting for transfers between devices, shards(): full_rows = lax.all_gather(hamiltonian, 'col', axis=1, tiled=True)  91.5 us
    all_gather x3, waiting for transfers between devices, stacked_from(): pieces = lax.all_gather(pieces, axes[k])  73.5 us
    all_to_all x1, waiting for transfers between devices, shards(): lax.all_to_all(outgoing.reshape(devices, capacity, block_size * block_siz...  48.6 us
    ppermute x1, waiting for transfers between devices, extended(): lax.ppermute(last, axis, up)  32.5 us
    unnamed x10, local copies, waits for them, and re-layouts  29 us
    dot_general x1, local copies, waits for them, and re-layouts, shards(): integrals = jnp.dot(gathering, received, precision=HIGHEST)  17.2 us
    dot_general x1, matrix products, shards(): jnp.dot(full_rows, gather_axes(masked_density, ROW, (0, 1, 2), 0), prefer...  15.7 us
  transfers between devices with their start and end apart: 8, of which 6 were waited for; matrix products, arithmetic and copies ran while one was open for 51% of the time, Pallas kernels for 0%

commit v1 on v0

v1 whole, which is shorter than its diff:
```python
import functools

import jax
import jax.numpy as jnp
from jax import lax
from jax.experimental import pallas as pl
from jax.experimental.pallas import tpu as pltpu
from jax.sharding import PartitionSpec as P

NATOMS = 64
NB = 128
CELLS = 384
ROWS = 16
COLS = 8
DEVICES = 128
ENTRIES = 64
ATOM_ROWS = 4
ATOM_COLS = 8
LOCAL = ATOM_ROWS * ATOM_COLS
TILE_R = 512
TILE_C = 1024
HALF = 256
MESH = pl.DeviceIdType.MESH
F32 = jnp.float32
BF16 = jnp.bfloat16
I32 = jnp.int32


def vmem():
    return pl.BlockSpec(memory_space=pltpu.VMEM)


def smem():
    return pl.BlockSpec(memory_space=pltpu.SMEM)


def hbm():
    return pl.BlockSpec(memory_space=pl.ANY)


def cube_kernel(
    own_off, left_off, right_off, pairs, live, pattern, corner, pot, density,
    own_out, right_out, left_out, entry_of, ids, masked, windows,
):
    lane = lax.broadcasted_iota(I32, (8, 128), 1)
    line = lax.broadcasted_iota(I32, (8, 128), 0)

    def cut(e, carry):
        for section, (off, first) in enumerate(
            ((own_off, 0), (own_off, 2), (right_off, 2), (left_off, 0))
        ):
            y = off[e, 1]
            z = off[e, 2]
            drop = y % 8
            turn = z % 128
            top = pl.multiple_of(y // 8 * 8, 8)
            below = pl.multiple_of(jnp.minimum(y // 8 + 1, 63) * 8, 8)
            near = pl.multiple_of(z // 128 * 128, 128)
            far = pl.multiple_of(jnp.minimum(z // 128 + 1, 3) * 128, 128)
            for p in range(2):
                quarter = [
                    [pot[first + p, pl.ds(r, 8), pl.ds(c, 128)] for c in (near, far)]
                    for r in (top, below)
                ]
                upper, lower = [jnp.where(lane >= turn, a, b) for a, b in quarter]
                window = jnp.where(line >= drop, upper, lower)
                window = pltpu.roll(window, (8 - drop) % 8, 0)
                window = pltpu.roll(window, (128 - turn) % 128, 1)
                start = pl.multiple_of(e * 16 + p * 8, 8)
                windows[section, pl.ds(start, 8), :] = window
        return carry

    lax.fori_loop(0, ENTRIES, cut, 0)

    def clear(d, carry):
        entry_of[d] = 0
        return carry

    lax.fori_loop(0, DEVICES, clear, 0)
    ids[...] = jnp.full(ids.shape, -1, I32)

    def place(e, carry):
        @pl.when(e < live[0])
        def _():
            i = pairs[e, 0]
            j = pairs[e, 1]
            owner = i // ATOM_ROWS * COLS + j // ATOM_COLS
            entry_of[owner] = e
            ids[owner] = jnp.full((1, 128), i % ATOM_ROWS * ATOM_COLS + j % ATOM_COLS, I32)

        return carry

    lax.fori_loop(0, ENTRIES, place, 0)

    rows = ENTRIES * 16
    at = lax.broadcasted_iota(I32, (128, 128), 0)
    to = lax.broadcasted_iota(I32, (128, 128), 1)
    spread = jnp.where(at == to % 8, 1.0, 0.0).astype(BF16)
    r = lax.broadcasted_iota(I32, (rows, 128), 0)
    c = lax.broadcasted_iota(I32, (rows, 128), 1)
    keep = (r % 16) == c // 8
    fold = jnp.where(
        lax.broadcasted_iota(I32, (ENTRIES, rows), 1) // 16
        == lax.broadcasted_iota(I32, (ENTRIES, rows), 0),
        1.0,
        0.0,
    ).astype(BF16)
    for section in range(4):
        wide = jnp.dot(windows[section].astype(BF16), spread, preferred_element_type=F32)
        wide = jnp.where(keep, wide, 0.0).astype(BF16)
        piece = jnp.dot(fold, wide, preferred_element_type=F32).astype(BF16)
        if section == 0:
            own_out[:, 0:128] = piece
        elif section == 1:
            own_out[:, 128:256] = piece
        elif section == 2:
            right_out[...] = piece
        else:
            left_out[...] = piece

    for i in range(ATOM_ROWS):
        for j in range(ATOM_COLS):
            on = pattern[corner[0] + i, corner[1] + j] > 0
            box = (slice(i * NB, (i + 1) * NB), slice(j * NB, (j + 1) * NB))

            @pl.when(on)
            def _():
                masked[box] = density[box]

            @pl.when(jnp.logical_not(on))
            def _():
                masked[box] = jnp.zeros((NB, NB), BF16)


def cut_cubes(own_off, left_off, right_off, pairs, live, pattern, corner, pot, density):
    return pl.pallas_call(
        cube_kernel,
        name="cut_cubes",
        out_shape=(
            jax.ShapeDtypeStruct((ENTRIES, 256), BF16),
            jax.ShapeDtypeStruct((ENTRIES, 128), BF16),
            jax.ShapeDtypeStruct((ENTRIES, 128), BF16),
            jax.ShapeDtypeStruct((DEVICES,), I32),
            jax.ShapeDtypeStruct((DEVICES, 1, 128), I32),
            jax.ShapeDtypeStruct((TILE_R, TILE_C), BF16),
        ),
        in_specs=[smem()] * 7 + [vmem()] * 2,
        out_specs=(vmem(), vmem(), vmem(), smem(), vmem(), vmem()),
        scratch_shapes=[pltpu.VMEM((4, ENTRIES * 16, 128), F32)],
        compiler_params=pltpu.CompilerParams(vmem_limit_bytes=48 << 20),
    )(own_off, left_off, right_off, pairs, live, pattern, corner, pot, density)


def place_of(index):
    return (index // COLS, index % COLS)


def exchange_kernel(
    entry_of, offx, own, to_right, to_left, ids, left, right,
    received, received_ids,
    left_v, right_v, low, high, cubes, blocks, table_sem, near_send, near_recv, send, recv, id_send, id_recv, local,
):
    me = lax.axis_index("row") * COLS + lax.axis_index("col")
    tables = (
        pltpu.make_async_copy(left, left_v, table_sem.at[0]),
        pltpu.make_async_copy(right, right_v, table_sem.at[1]),
    )
    for copy in tables:
        copy.start()
    near = (
        pltpu.make_async_remote_copy(
            to_right, low, near_send.at[0], near_recv.at[0], place_of((me + 1) % DEVICES), MESH
        ),
        pltpu.make_async_remote_copy(
            to_left, high, near_send.at[1], near_recv.at[1], place_of((me + DEVICES - 1) % DEVICES), MESH
        ),
    )
    for copy in near:
        copy.start()

    def id_copy(target):
        return pltpu.make_async_remote_copy(
            ids.at[target], received_ids.at[me], id_send, id_recv, place_of(target), MESH
        )

    def block_copy(target):
        return pltpu.make_async_remote_copy(
            blocks.at[target], received.at[me], send, recv, place_of(target), MESH
        )

    def send_id(k, carry):
        id_copy((me + k) % DEVICES).start()
        return carry

    lax.fori_loop(1, DEVICES, send_id, 0)
    own_id = pltpu.make_async_copy(ids.at[me], received_ids.at[me], local.at[0])
    own_id.start()
    for copy in near:
        copy.wait()
    line = jnp.concatenate([low[...], own[...], high[...]], axis=1).astype(F32)
    at = offx[...]
    cubes[...] = jnp.where(
        at == 0, line[:, 0:384], jnp.where(at == 1, line[:, 64:448], line[:, 128:512])
    )
    for copy in tables:
        copy.wait()

    def make(target):
        e = entry_of[target]
        weighted = left_v[e] * cubes[pl.ds(e, 1), :].astype(BF16)
        block = lax.dot_general(
            weighted, right_v[e], (((1,), (1,)), ((), ())), preferred_element_type=F32
        )
        blocks[target] = block.astype(BF16)

    make(me)
    make((me + 1) % DEVICES)

    def step(k, carry):
        make((me + k) % DEVICES)
        block_copy((me + k - 1) % DEVICES).start()
        return carry

    lax.fori_loop(2, DEVICES, step, 0)
    own_block = pltpu.make_async_copy(blocks.at[me], received.at[me], local.at[1])
    own_block.start()
    block_copy((me + DEVICES - 1) % DEVICES).start()
    own_id.wait()
    own_block.wait()
    all_but_one = pl.ds(0, DEVICES - 1)
    ids_done = pltpu.make_async_remote_copy(
        ids.at[all_but_one], received_ids.at[all_but_one], id_send, id_recv,
        place_of((me + 1) % DEVICES), MESH,
    )
    blocks_done = pltpu.make_async_remote_copy(
        blocks.at[all_but_one], received.at[all_but_one], send, recv,
        place_of((me + 1) % DEVICES), MESH,
    )
    ids_done.wait()
    blocks_done.wait()


def exchange(entry_of, offx, own, to_right, to_left, ids, left, right):
    return pl.pallas_call(
        exchange_kernel,
        name="exchange",
        out_shape=(
            jax.ShapeDtypeStruct((DEVICES, NB, NB), BF16),
            jax.ShapeDtypeStruct((DEVICES, 1, 128), I32),
        ),
        in_specs=[smem()] + [vmem()] * 5 + [hbm()] * 2,
        out_specs=(hbm(), hbm()),
        scratch_shapes=[
            pltpu.VMEM((ENTRIES, NB, CELLS), BF16),
            pltpu.VMEM((ENTRIES, NB, CELLS), BF16),
            pltpu.VMEM((ENTRIES, 128), BF16),
            pltpu.VMEM((ENTRIES, 128), BF16),
            pltpu.VMEM((ENTRIES, CELLS), F32),
            pltpu.VMEM((DEVICES, NB, NB), BF16),
            pltpu.SemaphoreType.DMA((2,)),
            pltpu.SemaphoreType.DMA((2,)),
            pltpu.SemaphoreType.DMA((2,)),
            pltpu.SemaphoreType.DMA,
            pltpu.SemaphoreType.DMA,
            pltpu.SemaphoreType.DMA,
            pltpu.SemaphoreType.DMA,
            pltpu.SemaphoreType.DMA((2,)),
        ],
        compiler_params=pltpu.CompilerParams(
            has_side_effects=True, vmem_limit_bytes=48 << 20
        ),
    )(entry_of, offx, own, to_right, to_left, ids, left, right)


def combine_kernel(pattern, corner, ids_hbm, received, core, ham, total, ids, sem):
    copy = pltpu.make_async_copy(ids_hbm, ids, sem)
    copy.start()
    total[...] = jnp.zeros(total.shape, F32)
    copy.wait()

    def add(s, carry):
        slot = ids[s, 0, 0]

        @pl.when(slot >= 0)
        def _():
            total[slot] += received[s].astype(F32)

        return carry

    lax.fori_loop(0, DEVICES, add, 0)
    for i in range(ATOM_ROWS):
        for j in range(ATOM_COLS):
            on = pattern[corner[0] + i, corner[1] + j] > 0
            box = (slice(i * NB, (i + 1) * NB), slice(j * NB, (j + 1) * NB))

            @pl.when(on)
            def _():
                ham[box] = (core[box].astype(F32) + total[i * ATOM_COLS + j]).astype(BF16)

            @pl.when(jnp.logical_not(on))
            def _():
                ham[box] = jnp.zeros((NB, NB), BF16)


def combine(pattern, corner, ids, received, core):
    return pl.pallas_call(
        combine_kernel,
        name="combine",
        out_shape=jax.ShapeDtypeStruct((TILE_R, TILE_C), BF16),
        in_specs=[smem(), smem(), hbm(), vmem(), vmem()],
        out_specs=vmem(),
        scratch_shapes=[
            pltpu.VMEM((LOCAL, NB, NB), F32),
            pltpu.SMEM((DEVICES, 1, 128), I32),
            pltpu.SemaphoreType.DMA,
        ],
        compiler_params=pltpu.CompilerParams(vmem_limit_bytes=48 << 20),
    )(pattern, corner, ids, received, core)


def product_kernel(ham, den, out, hbuf, dbuf, load, hsend, dsend, csend, hrecv, drecv):
    row = lax.axis_index("row")
    col = lax.axis_index("col")
    core = row % 2
    z = row // 2 % 4
    ylo = row // 8
    x = col // 2
    yhi = col % 2

    def col_of(x_, h_):
        return x_ % 4 * 2 + h_

    def row_of(l_, z_, c_):
        return l_ * 8 + z_ % 4 * 2 + c_

    def h_at(c, half):
        return hbuf.at[c, pl.ds(half * HALF, HALF), :]

    def d_at(r, half):
        start = pl.multiple_of(r % 2 * TILE_R + half * HALF, HALF)
        return dbuf.at[r // 2, pl.ds(start, HALF), :]

    sent = []

    def h_copy(c, half, target, sem):
        return pltpu.make_async_remote_copy(
            h_at(c, half), h_at(c, half), sem, hrecv.at[c, half], (row, target), MESH
        )

    def d_copy(r, half, target, sem):
        return pltpu.make_async_remote_copy(
            d_at(r, half), d_at(r, half), sem, drecv.at[r, half], (target, col), MESH
        )

    count = {"h": 0, "d": 0, "c": 0}

    def push(kind, make, block, half, target):
        sems = {"h": hsend, "d": dsend, "c": csend}[kind]
        copy = make(block, half, target, sems.at[count[kind]])
        count[kind] += 1
        copy.start()
        sent.append(copy)

    def h_wait(c, half):
        h_copy(c, half, col, hsend.at[0]).wait_recv()

    def d_wait(r, half):
        d_copy(r, half, row, dsend.at[0]).wait_recv()

    first = (
        pltpu.make_async_copy(ham, hbuf.at[col], load.at[0]),
        pltpu.make_async_copy(
            den, dbuf.at[row // 2, pl.ds(pl.multiple_of(core * TILE_R, TILE_R), TILE_R), :], load.at[1]
        ),
    )
    for copy in first:
        copy.start()
    for copy in first:
        copy.wait()

    other_core = row_of(ylo, z, 1 - core)
    h_partner = col_of(x, 1 - yhi)
    d_partner = row_of(1 - ylo, z, core)
    x_up, x_down = col_of(x + 1, yhi), col_of(x + 3, yhi)
    z_up, z_down = row_of(ylo, z + 1, core), row_of(ylo, z + 3, core)

    def h_ring(h_):
        me_ = col_of(x, h_)
        for n in range(2):
            push("h", h_copy, me_, n, x_up)
            push("h", h_copy, me_, 1 - n, x_down)

    def d_ring(l_):
        me_ = row_of(l_, z, core)
        for n in range(2):
            push("d", d_copy, me_, n, z_up)
            push("d", d_copy, me_, 1 - n, z_down)

    def share(r, half):
        push("c", d_copy, r, half, other_core)

    def h_forward(h_):
        h_wait(col_of(x + 3, h_), 0)
        push("h", h_copy, col_of(x + 3, h_), 0, x_up)
        h_wait(col_of(x + 1, h_), 1)
        push("h", h_copy, col_of(x + 1, h_), 1, x_down)

    def d_forward(l_):
        down, up = row_of(l_, z + 3, core), row_of(l_, z + 1, core)
        d_wait(down, 0)
        push("d", d_copy, down, 0, z_up)
        d_wait(up, 1)
        push("d", d_copy, up, 1, z_down)
        share(down, 0)
        share(up, 1)

    def h_rest(h_):
        h_wait(col_of(x + 3, h_), 1)
        h_wait(col_of(x + 1, h_), 0)

    def h_far(h_):
        h_wait(col_of(x + 2, h_), 0)
        h_wait(col_of(x + 2, h_), 1)

    def d_rest(l_):
        down, up = row_of(l_, z + 3, core), row_of(l_, z + 1, core)
        d_wait(down, 1)
        d_wait(up, 0)
        share(down, 1)
        share(up, 0)

    def d_far(l_):
        far = row_of(l_, z + 2, core)
        for n in range(2):
            d_wait(far, n)
            share(far, n)

    def d_other(l_, z_):
        r = row_of(l_, z_, 1 - core)
        for n in range(2):
            d_wait(r, n)

    def multiply(l_, z_, start):
        k = l_ * 4 + z_

        def tile(n, carry):
            columns = pl.ds(pl.multiple_of(n * 256, 256), 256)
            part = jnp.dot(hbuf[k], dbuf[k, :, columns], preferred_element_type=F32)
            if start:
                out[:, columns] = part
            else:
                out[:, columns] += part
            return carry

        lax.fori_loop(0, TILE_C // 256, tile, 0)

    h_ring(yhi)
    for n in range(2):
        push("h", h_copy, col, n, h_partner)
    d_ring(ylo)
    for n in range(2):
        push("d", d_copy, row, n, d_partner)
    for n in range(2):
        share(row, n)

    h_forward(yhi)
    d_forward(ylo)
    for n in range(2):
        h_wait(h_partner, n)
    h_ring(1 - yhi)
    for n in range(2):
        d_wait(d_partner, n)
    d_ring(1 - ylo)
    for n in range(2):
        share(d_partner, n)
    h_rest(yhi)
    d_rest(ylo)
    h_far(yhi)
    d_far(ylo)
    for n in range(4):
        d_other(ylo, z + n)
    multiply(ylo, yhi, True)
    multiply(ylo, 2 + yhi, False)
    h_forward(1 - yhi)
    d_forward(1 - ylo)
    h_rest(1 - yhi)
    d_rest(1 - ylo)
    h_far(1 - yhi)
    multiply(ylo, 1 - yhi, False)
    multiply(ylo, 3 - yhi, False)
    d_far(1 - ylo)
    for n in range(4):
        d_other(1 - ylo, z + n)
    for n in range(4):
        multiply(1 - ylo, n, False)
    for copy in sent:
        copy.wait_send()


def multiply_all(ham, den):
    return pl.pallas_call(
        product_kernel,
        name="product",
        out_shape=jax.ShapeDtypeStruct((TILE_R, TILE_C), F32),
        in_specs=[hbm(), hbm()],
        out_specs=vmem(),
        scratch_shapes=[
            pltpu.VMEM((COLS, TILE_R, TILE_C), BF16),
            pltpu.VMEM((COLS, 2 * TILE_R, TILE_C), BF16),
            pltpu.SemaphoreType.DMA((2,)),
            pltpu.SemaphoreType.DMA((16,)),
            pltpu.SemaphoreType.DMA((16,)),
            pltpu.SemaphoreType.DMA((16,)),
            pltpu.SemaphoreType.DMA((COLS, 2)),
            pltpu.SemaphoreType.DMA((ROWS, 2)),
        ],
        compiler_params=pltpu.CompilerParams(
            has_side_effects=True, vmem_limit_bytes=56 << 20
        ),
    )(ham, den)


def shards(
    potential, basis_left, basis_right, core_matrix, density, pattern, pair_atoms, cube_offsets, live_count
):
    up = [(i, (i + 1) % DEVICES) for i in range(DEVICES)]
    left_off = lax.ppermute(cube_offsets, ("row", "col"), up)
    right_off = lax.ppermute(cube_offsets, ("row", "col"), [(b, a) for a, b in up])
    corner = jnp.stack([lax.axis_index("row") * ATOM_ROWS, lax.axis_index("col") * ATOM_COLS]).astype(I32)
    own, to_right, to_left, entry_of, ids, masked = cut_cubes(
        cube_offsets, left_off, right_off, pair_atoms, live_count, pattern, corner, potential, density
    )
    received, received_ids = exchange(
        entry_of, cube_offsets[:, 0:1], own, to_right, to_left, ids, basis_left, basis_right
    )
    ham = combine(pattern, corner, received_ids, received, core_matrix)
    return ham, multiply_all(ham, masked)


def solution(mesh):
    flat = ("row", "col")
    tile = P("row", "col")
    placed = (
        P(flat, None, None),
        P(flat, None, None),
        P(flat, None, None),
        tile,
        tile,
        P(),
        P(flat, None),
        P(flat, None),
        P(flat),
    )
    return jax.shard_map(
        shards, mesh=mesh, in_specs=placed, out_specs=(tile, tile), check_vma=False
    )
```

time: 635 us -> 224 us (0.35)
  local copies, waits for them, and re-layouts: 283 us -> 6.7 us
  waiting for transfers between devices: 251 us -> 5.76 us
  Pallas kernels: 0 us -> 203 us
  matrix products: 35.6 us -> 0 us
  other arithmetic: 21.7 us -> 0.07 us
  starting transfers between devices: 23.1 us -> 6.53 us
  between operations: 14.6 us -> 1.35 us
    gather x193 -> x0, local copies, waits for them, and re-layouts: 220 us -> none
    pallas_call x0 -> x4, Pallas kernels: none -> 203 us  [the longest x1 108 us: multiply_all(): pl.pallas_call(product_kernel, name='product', out_shape=jax.ShapeDtypeSt...]
    all_gather x4 -> x0, waiting for transfers between devices: 165 us -> none  [the longest x1 91.5 us: shards(): full_rows = lax.all_gather(hamiltonian, 'col', axis=1, tiled=True)]
    all_to_all x2 -> x0, waiting for transfers between devices: 48.6 us -> none  [the longest x1 48.6 us: shards(): lax.all_to_all(outgoing.reshape(devices, capacity, block_size * block_siz...]
    dot_general x4 -> x0, matrix products: 35.6 us -> none  [the longest x1 15.7 us: shards(): jnp.dot(full_rows, gather_axes(masked_density, ROW, (0, 1, 2), 0), prefer...]
    ppermute x2, waiting for transfers between devices: 37.2 us -> 5.76 us  [the longest x1 5.76 us: shards(): left_off = lax.ppermute(cube_offsets, ('row', 'col'), up)]
    unnamed x10 -> x11, local copies, waits for them, and re-layouts: 29 us -> 6.7 us
    dot_general x1 -> x0, local copies, waits for them, and re-layouts: 17.2 us -> none  [shards(): integrals = jnp.dot(gathering, received, precision=HIGHEST)]
  transfers between devices with their start and end apart: 8 -> 2, of which waited for: 6 -> 1; matrix products, arithmetic and copies ran while one was open for 51% -> 0% of each run, Pallas kernels for 0% -> 0%
where the time goes in v1:
time: 224 us; the launch traced here: 223 us
  Pallas kernels  203 us (91%)
  local copies, waits for them, and re-layouts  6.7 us (3%)
  starting transfers between devices  6.53 us (3%)
  waiting for transfers between devices  5.76 us (3%)
    pallas_call x1, Pallas kernels, multiply_all(): pl.pallas_call(product_kernel, name='product', out_shape=jax.ShapeDtypeSt...  108 us
    pallas_call x1, Pallas kernels, exchange(): pl.pallas_call(exchange_kernel, name='exchange', out_shape=(jax.ShapeDtyp...  71.1 us
    pallas_call x1, Pallas kernels, cut_cubes(): pl.pallas_call(cube_kernel, name='cut_cubes', out_shape=(jax.ShapeDtypeSt...  17.5 us
    unnamed x11, local copies, waits for them, and re-layouts  6.7 us
    pallas_call x1, Pallas kernels, combine(): pl.pallas_call(combine_kernel, name='combine', out_shape=jax.ShapeDtypeSt...  6.65 us
    ppermute x1, starting transfers between devices, shards(): lax.ppermute(cube_offsets, ('row', 'col'), [(b, a) for a, b in up])  6.53 us
    ppermute x1, waiting for transfers between devices, shards(): left_off = lax.ppermute(cube_offsets, ('row', 'col'), up)  5.76 us
  transfers between devices with their start and end apart: 2, of which 1 were waited for; matrix products, arithmetic and copies ran while one was open for 0% of the time, Pallas kernels for 0%

profile of v1, /device:TPU:1, one launch (start us, length us, event | category | flops | bytes accessed | tf_op | source)
XLA Modules:
  0.0 223.4 jit_solution(7072453397566291853)
XLA Ops:
  0.6 0.8 copy.13.own_off
  1.4 6.5 %collective-permute-start.1 = (s32[64,3]{1,0:T(8,128)S(1)}, s32[64,3]{1,0:T(8,128)S(1)}, u32[]{:S(2)}, u32[]{:S(2)}) collective-permute-start(s32[64,3]{1,0:T(8,128)S(1)} %copy.13.own_off), channel_id=1, source_target_pairs={{1,0},{2,1},{3,2},{4,3},{5,4},{6,5},{7,6},{8,7},{9,8},{10,9},{11,1... | collective-permute-start | bytes 2312 | tf_op jit(solution)/shard_map/ppermute | solution.py:528
  7.9 0.0 collective-permute-start
  7.9 0.1 pad_add_fusion.corner
  8.7 0.8 copy.14.pairs
  9.4 0.0 collective-permute-done.1.right_off
  9.4 5.8 %collective-permute-done.left_off = s32[64,3]{1,0:T(8,128)S(1)} collective-permute-done((s32[64,3]{1,0:T(8,128)S(1)}, s32[64,3]{1,0:T(8,128)S(1)}, u32[]{:S(2)}, u32[]{:S(2)}) %collective-permute-start) | collective-permute-done | bytes 800 | tf_op jit(solution)/shard_map/ppermute | solution.py:527
  15.2 0.0 copy-start.1
  15.2 1.2 copy-done.1
  16.4 0.0 copy-start.3
  16.4 0.8 copy-done.3
  17.2 17.5 %cut_cubes.1 = (bf16[64,256]{1,0:T(8,128)(2,1)S(1)}, bf16[64,128]{1,0:T(8,128)(2,1)S(1)}, bf16[64,128]{1,0:T(8,128)(2,1)S(1)}, s32[128]{0:T(128)S(1)}, s32[128,1...) custom-call(s32[64,3]{1,0:T(8,128)S(1)} %copy.13.own_off, s32[64,3]{1,0:T(8,128)S(1)} %collective-permute-done.left_off, ...), custom_call_target="tpu_custom_call" | custom-call | tf_op jit(solution)/shard_map/cut_cubes/pallas_call | solution.py:136
  34.7 0.0 copy-start.2
  34.7 0.0 copy-start
  34.7 71.1 %exchange.1 = (bf16[128,128,128]{2,1,0:T(8,128)(2,1)S(1)}, s32[128,1,128]{2,1,0:T(1,128)S(1)}) custom-call(s32[128]{0:T(128)S(1)} %get-tuple-element.10.entry_of, s32[64,1]{1,0:T(8,128)S(1)} %bitcast.3, bf16[64,256]{1,0:T(8,128)(2,1)S(1)} %get-tuple-element.11.own, bf16[64,128]{1,0:T(8,128)(2,1)S(1)} %get-tuple-element.12.to_right, ...), custom_call_target="tpu_custom_call" | custom-call | tf_op jit(solution)/shard_map/exchange/pallas_call | solution.py:244
  105.8 0.0 copy-done.2
  105.8 0.0 copy-done
  105.8 6.7 %combine.1.ham = bf16[512,1024]{1,0:T(8,128)(2,1)} custom-call(s32[64,64]{1,0:T(8,128)S(1)} %copy-done.3, s32[2]{0:T(128)S(1)} %pad_add_fusion.corner, s32[128,1,128]{2,1,0:T(1,128)S(1)} %get-tuple-element.15.ids_hbm, bf16[128,128,128]{2,1,0:T(8,128)(2,1)S(1)} %get-tuple-element.16.received, bf16[512,1024]{1,0:T(8,128)(2,1)S(1)} %copy-done), custom_call_target="tpu_custom_call" | custom-call | tf_op jit(solution)/shard_map/combine/pallas_call | solution.py:306
  112.5 107.8 %product.1 = f32[512,1024]{1,0:T(8,128)} custom-call(bf16[512,1024]{1,0:T(8,128)(2,1)} %combine.1.ham, bf16[512,1024]{1,0:T(8,128)(2,1)} %copy-done.2), custom_call_target="tpu_custom_call" | custom-call | tf_op jit(solution)/shard_map/product/pallas_call | solution.py:501
  220.3 3.2 %copy.18 = f32[512,1024]{1,0:T(8,128)} copy(f32[512,1024]{1,0:T(8,128)} %product.1) | data formatting | bytes 4194304
Async XLA Ops:
  1.4 8.0 %collective-permute-start.1 = (s32[64,3]{1,0:T(8,128)S(1)}, s32[64,3]{1,0:T(8,128)S(1)}, u32[]{:S(2)}, u32[]{:S(2)}) collective-permute-start(s32[64,3]{1,0:T(8,128)S(1)} %copy.13.own_off), channel_id=1, source_target_pairs={{1,0},{2,1},{3,2},{4,3},{5,4},{6,5},{7,6},{8,7},{9,8},{10,9},{11,1... | collective-permute-start | bytes 2312 | tf_op jit(solution)/shard_map/ppermute | solution.py:528
  7.9 7.3 %collective-permute-start = (s32[64,3]{1,0:T(8,128)S(1)}, s32[64,3]{1,0:T(8,128)S(1)}, u32[]{:S(2)}, u32[]{:S(2)}) collective-permute-start(s32[64,3]{1,0:T(8,128)S(1)} %copy.13.own_off), channel_id=1, source_target_pairs={{0,1},{1,2},{2,3},{3,4},{4,5},{5,6},{6,7},{7,8},{8,9},{9,10},{10,1... | collective-permute-start | bytes 2312 | tf_op jit(solution)/shard_map/ppermute | solution.py:527
  15.2 1.2 copy-start.1
  16.4 0.8 copy-start.3
  34.7 71.2 %copy-start.2 = (bf16[512,1024]{1,0:T(8,128)(2,1)}, bf16[512,1024]{1,0:T(8,128)(2,1)S(1)}, u32[]{:S(2)}) copy-start(bf16[512,1024]{1,0:T(8,128)(2,1)S(1)} %get-tuple-element.17.den) | copy-start | bytes 3145732
  34.7 71.2 %copy-start = (bf16[512,1024]{1,0:T(8,128)(2,1)S(1)}, bf16[512,1024]{1,0:T(8,128)(2,1)}, u32[]{:S(2)}) copy-start(bf16[512,1024]{1,0:T(8,128)(2,1)} %core.1) | copy-start | bytes 3145732

commit v2 on v1

v2 whole, which is shorter than its diff:
```python
import functools

import jax
import jax.numpy as jnp
from jax import lax
from jax.experimental import pallas as pl
from jax.experimental.pallas import tpu as pltpu
from jax.sharding import PartitionSpec as P

NATOMS = 64
NB = 128
CELLS = 384
ROWS = 16
COLS = 8
DEVICES = 128
ENTRIES = 64
ATOM_ROWS = 4
ATOM_COLS = 8
LOCAL = ATOM_ROWS * ATOM_COLS
TILE_R = 512
TILE_C = 1024
HALF = 256
STRIDE = 51
SPLIT = 40
MESH = pl.DeviceIdType.MESH
F32 = jnp.float32
BF16 = jnp.bfloat16
I32 = jnp.int32


def vmem():
    return pl.BlockSpec(memory_space=pltpu.VMEM)


def smem():
    return pl.BlockSpec(memory_space=pltpu.SMEM)


def hbm():
    return pl.BlockSpec(memory_space=pl.ANY)


def place_of(index):
    return (index // COLS, index % COLS)


def exchange_kernel(
    offsets, pairs, live, pattern, pot, density, left, right,
    received, received_ids, near_den,
    pot_v, den_v, left_v, right_v, windows, own_off, other_off, off_s, table, table_s, ids,
    to_right, to_left, low, high, cubes, blocks,
    load_sem, off_send, off_recv, copy_sem, near_send, near_recv, send, recv, id_send, id_recv,
    den_send, den_recv, local,
):
    row = lax.axis_index("row")
    col = lax.axis_index("col")
    me = row * COLS + col
    above = place_of((me + 1) % DEVICES)
    below = place_of((me + DEVICES - 1) % DEVICES)

    loads = [
        pltpu.make_async_copy(a, b, load_sem.at[n])
        for n, (a, b) in enumerate(((density, den_v), (left, left_v), (right, right_v)))
    ]
    pot_loads = [
        pltpu.make_async_copy(
            pot.at[:, :, :, pl.ds(n * 128, 128)], pot_v.at[n], load_sem.at[n + 3]
        )
        for n in range(4)
    ]
    for copy in loads[:1] + pot_loads + loads[1:]:
        copy.start()
    barrier = pltpu.get_barrier_semaphore()

    def greet(k, carry):
        pl.semaphore_signal(
            barrier, inc=1, device_id=place_of((me + k) % DEVICES), device_id_type=MESH
        )
        return carry

    lax.fori_loop(1, DEVICES, greet, 0)

    own_off[...] = jnp.zeros((8, 128), I32)
    own_off[0:1, 0:ENTRIES] = offsets[0:1, :]
    own_y = offsets[1:2, :]
    own_z = offsets[2:3, :]
    for n, value in enumerate(
        (
            own_y >> 3,
            jnp.minimum((own_y >> 3) + 1, 63),
            own_z >> 7,
            jnp.minimum((own_z >> 7) + 1, 3),
            own_y & 7,
            own_z & 127,
        )
    ):
        own_off[n + 1 : n + 2, 0:ENTRIES] = value
    own_scalars = pltpu.make_async_copy(own_off, off_s.at[0], copy_sem.at[0])
    own_scalars.start()

    entry = lax.broadcasted_iota(I32, (ENTRIES, ENTRIES), 0)
    eye = entry == lax.broadcasted_iota(I32, (ENTRIES, ENTRIES), 1)

    def upright(line):
        return jnp.sum(jnp.where(eye, line, 0), axis=1, keepdims=True)

    first = pairs[0:1, :]
    second = pairs[1:2, :]
    owner = upright(first // ATOM_ROWS * COLS + second // ATOM_COLS)
    place = upright(first % ATOM_ROWS * ATOM_COLS + second % ATOM_COLS)
    at_x = upright(offsets[0:1, :])
    ordinal = lax.broadcasted_iota(I32, (ENTRIES, DEVICES), 0)
    target_of = lax.broadcasted_iota(I32, (ENTRIES, DEVICES), 1)
    named = jnp.logical_and(owner == target_of, ordinal < live[0])
    table[...] = jnp.zeros((8, 128), I32)
    table[0:1, :] = jnp.sum(jnp.where(named, ordinal, 0), axis=0, keepdims=True)
    table[1:2, :] = jnp.sum(jnp.where(named, place + 1, 0), axis=0, keepdims=True) - 1
    table_scalars = pltpu.make_async_copy(table, table_s, copy_sem.at[1])
    table_scalars.start()

    loads[0].wait()
    for i in range(ATOM_ROWS):
        for j in range(ATOM_COLS):
            on = jnp.full((NB, NB), pattern[row * ATOM_ROWS + i, col * ATOM_COLS + j], I32) > 0
            box = (slice(i * NB, (i + 1) * NB), slice(j * NB, (j + 1) * NB))
            den_v[box] = jnp.where(on, den_v[box].astype(F32), 0.0).astype(BF16)
    keep_den = pltpu.make_async_copy(den_v, near_den.at[0], local.at[2])
    keep_den.start()

    lane = lax.broadcasted_iota(I32, (8, 128), 1)
    line = lax.broadcasted_iota(I32, (8, 128), 0)

    def cut(source, e, planes):
        y_tiles = (off_s[source, 1, e], off_s[source, 2, e])
        z_tiles = (off_s[source, 3, e], off_s[source, 4, e])
        drop = off_s[source, 5, e]
        turn = off_s[source, 6, e]
        kept = ((lane - turn) & 127) < 8
        for section, plane in planes:
            for p in range(2):
                quarter = [
                    [pot_v[zt, plane + p, yt] for zt in z_tiles] for yt in y_tiles
                ]
                upper, lower = [jnp.where(lane >= turn, a, b) for a, b in quarter]
                window = jnp.where(jnp.logical_and(line >= drop, kept), upper, 0.0)
                window = jnp.where(jnp.logical_and(line < drop, kept), lower, window)
                start = pl.multiple_of(e * 16 + p * 8, 8)
                windows[section, pl.ds(start, 8), :] = window

    def cut_own(e, carry):
        for n in range(4):
            cut(0, e * 4 + n, ((0, 0), (1, 2)))
        return carry

    def cut_others(e, carry):
        for n in range(4):
            cut(1, e * 4 + n, ((2, 2),))
            cut(2, e * 4 + n, ((3, 0),))
        return carry

    pl.semaphore_wait(barrier, DEVICES - 1)
    off_copies = (
        pltpu.make_async_remote_copy(
            own_off, other_off.at[0], off_send.at[0], off_recv.at[0], below, MESH
        ),
        pltpu.make_async_remote_copy(
            own_off, other_off.at[1], off_send.at[1], off_recv.at[1], above, MESH
        ),
    )
    for copy in off_copies:
        copy.start()

    def den_copy(slot, half, device):
        part = pl.ds(half * HALF, HALF)
        return pltpu.make_async_remote_copy(
            den_v.at[part, :], near_den.at[slot, part, :],
            den_send.at[slot, half], den_recv.at[slot, half], device, MESH,
        )

    z = row // 2 % 4
    base = row - z * 2
    den_targets = (
        (1, ((row + 8) % ROWS, col)),
        (2, (base + (z + 1) % 4 * 2, col)),
        (3, (base + (z + 3) % 4 * 2, col)),
    )
    den_copies = [[den_copy(slot, half, device) for slot, device in den_targets] for half in range(2)]
    for copy in den_copies[0]:
        copy.start()

    own_scalars.wait()
    for copy in pot_loads:
        copy.wait()
    lax.fori_loop(0, ENTRIES // 4, cut_own, 0)

    at = lax.broadcasted_iota(I32, (128, 128), 0)
    to = lax.broadcasted_iota(I32, (128, 128), 1)
    spread = jnp.where(at % 8 == to % 8, 1.0, 0.0).astype(BF16)
    rows = ENTRIES * 16
    at_row = lax.broadcasted_iota(I32, (rows, 128), 0)
    at_lane = lax.broadcasted_iota(I32, (rows, 128), 1)
    right_plane = at_row // 8 % 2 == at_lane // 64
    fold = jnp.where(
        lax.broadcasted_iota(I32, (ENTRIES, rows), 1) // 16
        == lax.broadcasted_iota(I32, (ENTRIES, rows), 0),
        1.0,
        0.0,
    ).astype(BF16)
    unfold = jnp.where(
        lax.broadcasted_iota(I32, (rows, ENTRIES), 0) // 16
        == lax.broadcasted_iota(I32, (rows, ENTRIES), 1),
        1.0,
        0.0,
    ).astype(BF16)
    cell = lax.broadcasted_iota(I32, (ENTRIES, 128), 1) % 8

    def pieces(sections, place_yz):
        drop = upright(place_yz[0:1, :]).astype(F32)
        turn = upright(place_yz[1:2, :])
        drop_rows = jnp.dot(
            unfold, jnp.broadcast_to(drop, (ENTRIES, 128)).astype(BF16), preferred_element_type=F32
        ).astype(I32)
        keep = jnp.logical_and(((at_row - drop_rows) & 7) == at_lane // 8 % 8, right_plane)
        made = []
        for section in sections:
            wide = jnp.dot(windows[section].astype(BF16), spread, preferred_element_type=F32)
            wide = jnp.where(keep, wide, 0.0).astype(BF16)
            piece = jnp.dot(fold, wide, preferred_element_type=F32)
            for s in (1, 2, 4):
                moved = jnp.where(
                    cell + s < 8, pltpu.roll(piece, 128 - s, 1), pltpu.roll(piece, 8 - s, 1)
                )
                piece = jnp.where((turn & s) > 0, moved, piece)
            made.append(piece)
        return made

    own_piece = pieces((0, 1), own_off[5:7, 0:ENTRIES])
    for copy in off_copies:
        copy.wait()
    other_scalars = [
        pltpu.make_async_copy(other_off.at[n], off_s.at[n + 1], copy_sem.at[n + 2]) for n in range(2)
    ]
    for copy in other_scalars:
        copy.start()
    table_scalars.wait()

    def write_id(d, carry):
        ids[d] = jnp.full((1, 128), table_s[1, d], I32)
        return carry

    lax.fori_loop(0, DEVICES, write_id, 0)
    for copy in other_scalars:
        copy.wait()
    lax.fori_loop(0, ENTRIES // 4, cut_others, 0)
    to_right[...] = pieces((2,), other_off[0, 5:7, 0:ENTRIES])[0].astype(BF16)
    to_left[...] = pieces((3,), other_off[1, 5:7, 0:ENTRIES])[0].astype(BF16)
    near = (
        pltpu.make_async_remote_copy(to_right, low, near_send.at[0], near_recv.at[0], above, MESH),
        pltpu.make_async_remote_copy(to_left, high, near_send.at[1], near_recv.at[1], below, MESH),
    )
    for copy in near:
        copy.start()

    def id_copy(target):
        return pltpu.make_async_remote_copy(
            ids.at[target], received_ids.at[me], id_send, id_recv, place_of(target), MESH
        )

    def block_copy(target):
        return pltpu.make_async_remote_copy(
            blocks.at[target], received.at[me], send, recv, place_of(target), MESH
        )

    def send_id(k, carry):
        id_copy((me + k) % DEVICES).start()
        return carry

    lax.fori_loop(1, DEVICES, send_id, 0)
    own_id = pltpu.make_async_copy(ids.at[me], received_ids.at[me], local.at[0])
    own_id.start()
    for copy in near:
        copy.wait()
    whole = jnp.concatenate(
        [low[...].astype(F32), own_piece[0], own_piece[1], high[...].astype(F32)], axis=1
    )
    cubes[...] = jnp.where(
        at_x == 0, whole[:, 0:384], jnp.where(at_x == 1, whole[:, 64:448], whole[:, 128:512])
    )
    for copy in loads[1:]:
        copy.wait()

    def make(target):
        e = table_s[0, target]
        weighted = left_v[e] * cubes[pl.ds(e, 1), :].astype(BF16)
        block = lax.dot_general(
            weighted, right_v[e], (((1,), (1,)), ((), ())), preferred_element_type=F32
        )
        blocks[target] = block.astype(BF16)

    def target_at(k):
        return (me + k * STRIDE) % DEVICES

    make(target_at(1))

    def step(k, carry):
        make(target_at(k))
        block_copy(target_at(k - 1)).start()
        return carry

    lax.fori_loop(2, SPLIT, step, 0)
    for copy in den_copies[1]:
        copy.start()
    lax.fori_loop(SPLIT, DEVICES, step, 0)
    make(me)
    block_copy(target_at(DEVICES - 1)).start()
    own_block = pltpu.make_async_copy(blocks.at[me], received.at[me], local.at[1])
    own_block.start()
    own_id.wait()
    keep_den.wait()
    own_block.wait()
    all_but_one = pl.ds(0, DEVICES - 1)
    ids_done = pltpu.make_async_remote_copy(
        ids.at[all_but_one], received_ids.at[all_but_one], id_send, id_recv, above, MESH
    )
    blocks_done = pltpu.make_async_remote_copy(
        blocks.at[all_but_one], received.at[all_but_one], send, recv, above, MESH
    )
    ids_done.wait()
    for half in range(2):
        for copy in den_copies[half]:
            copy.wait()
    blocks_done.wait()


def exchange(offsets, pairs, live, pattern, pot, density, left, right):
    dma = pltpu.SemaphoreType.DMA
    return pl.pallas_call(
        exchange_kernel,
        name="exchange",
        out_shape=(
            jax.ShapeDtypeStruct((DEVICES, NB, NB), BF16),
            jax.ShapeDtypeStruct((DEVICES, 1, 128), I32),
            jax.ShapeDtypeStruct((4, TILE_R, TILE_C), BF16),
        ),
        in_specs=[vmem(), vmem(), smem(), smem()] + [hbm()] * 4,
        out_specs=(hbm(), hbm(), hbm()),
        scratch_shapes=[
            pltpu.VMEM((4, 4, 64, 8, 128), F32),
            pltpu.VMEM((TILE_R, TILE_C), BF16),
            pltpu.VMEM((ENTRIES, NB, CELLS), BF16),
            pltpu.VMEM((ENTRIES, NB, CELLS), BF16),
            pltpu.VMEM((4, ENTRIES * 16, 128), F32),
            pltpu.VMEM((8, 128), I32),
            pltpu.VMEM((2, 8, 128), I32),
            pltpu.SMEM((3, 8, 128), I32),
            pltpu.VMEM((8, 128), I32),
            pltpu.SMEM((8, 128), I32),
            pltpu.VMEM((DEVICES, 1, 128), I32),
            pltpu.VMEM((ENTRIES, 128), BF16),
            pltpu.VMEM((ENTRIES, 128), BF16),
            pltpu.VMEM((ENTRIES, 128), BF16),
            pltpu.VMEM((ENTRIES, 128), BF16),
            pltpu.VMEM((ENTRIES, CELLS), F32),
            pltpu.VMEM((DEVICES, NB, NB), BF16),
            dma((7,)), dma((2,)), dma((2,)), dma((4,)), dma((2,)), dma((2,)),
            dma, dma, dma, dma, dma((4, 2)), dma((4, 2)), dma((3,)),
        ],
        compiler_params=pltpu.CompilerParams(
            has_side_effects=True, vmem_limit_bytes=48 << 20, collective_id=0
        ),
    )(offsets, pairs, live, pattern, pot, density, left, right)


def combine_kernel(pattern, corner, ids_hbm, received, core, ham, total, ids, sem):
    copy = pltpu.make_async_copy(ids_hbm, ids, sem)
    copy.start()
    total[...] = jnp.zeros(total.shape, F32)
    copy.wait()

    def add(s, carry):
        slot = ids[s, 0, 0]

        @pl.when(slot >= 0)
        def _():
            total[slot] += received[s].astype(F32)

        return carry

    lax.fori_loop(0, DEVICES, add, 0)
    for i in range(ATOM_ROWS):
        for j in range(ATOM_COLS):
            on = pattern[corner[0] + i, corner[1] + j] > 0
            box = (slice(i * NB, (i + 1) * NB), slice(j * NB, (j + 1) * NB))

            @pl.when(on)
            def _():
                ham[box] = (core[box].astype(F32) + total[i * ATOM_COLS + j]).astype(BF16)

            @pl.when(jnp.logical_not(on))
            def _():
                ham[box] = jnp.zeros((NB, NB), BF16)


def combine(pattern, corner, ids, received, core):
    return pl.pallas_call(
        combine_kernel,
        name="combine",
        out_shape=jax.ShapeDtypeStruct((TILE_R, TILE_C), BF16),
        in_specs=[smem(), smem(), hbm(), vmem(), vmem()],
        out_specs=vmem(),
        scratch_shapes=[
            pltpu.VMEM((LOCAL, NB, NB), F32),
            pltpu.SMEM((DEVICES, 1, 128), I32),
            pltpu.SemaphoreType.DMA,
        ],
        compiler_params=pltpu.CompilerParams(vmem_limit_bytes=48 << 20),
    )(pattern, corner, ids, received, core)


def product_kernel(ham, den, out, hbuf, dbuf, load, hsend, dsend, csend, hrecv, drecv):
    row = lax.axis_index("row")
    col = lax.axis_index("col")
    core = row % 2
    z = row // 2 % 4
    ylo = row // 8
    x = col // 2
    yhi = col % 2

    def col_of(x_, h_):
        return x_ % 4 * 2 + h_

    def row_of(l_, z_, c_):
        return l_ * 8 + z_ % 4 * 2 + c_

    def h_at(c, half):
        return hbuf.at[c, pl.ds(half * HALF, HALF), :]

    def d_at(r, half):
        start = pl.multiple_of(r % 2 * TILE_R + half * HALF, HALF)
        return dbuf.at[r // 2, pl.ds(start, HALF), :]

    sent = []

    def h_copy(c, half, target, sem):
        return pltpu.make_async_remote_copy(
            h_at(c, half), h_at(c, half), sem, hrecv.at[c, half], (row, target), MESH
        )

    def d_copy(r, half, target, sem):
        return pltpu.make_async_remote_copy(
            d_at(r, half), d_at(r, half), sem, drecv.at[r, half], (target, col), MESH
        )

    count = {"h": 0, "d": 0, "c": 0}

    def push(kind, make, block, half, target):
        sems = {"h": hsend, "d": dsend, "c": csend}[kind]
        copy = make(block, half, target, sems.at[count[kind]])
        count[kind] += 1
        copy.start()
        sent.append(copy)

    def h_wait(c, half):
        h_copy(c, half, col, hsend.at[0]).wait_recv()

    def d_wait(r, half):
        d_copy(r, half, row, dsend.at[0]).wait_recv()

    other_core = row_of(ylo, z, 1 - core)
    h_partner = col_of(x, 1 - yhi)
    d_partner = row_of(1 - ylo, z, core)
    x_up, x_down = col_of(x + 1, yhi), col_of(x + 3, yhi)
    z_up, z_down = row_of(ylo, z + 1, core), row_of(ylo, z + 3, core)
    h_up, h_down = col_of(x + 1, 1 - yhi), col_of(x + 3, 1 - yhi)
    d_up, d_down = row_of(1 - ylo, z + 1, core), row_of(1 - ylo, z + 3, core)

    first = [pltpu.make_async_copy(ham, hbuf.at[col], load.at[0])] + [
        pltpu.make_async_copy(
            den.at[n],
            dbuf.at[r // 2, pl.ds(pl.multiple_of(core * TILE_R, TILE_R), TILE_R), :],
            load.at[n + 1],
        )
        for n, r in enumerate((row, d_partner, z_down, z_up))
    ]
    for copy in first:
        copy.start()
    barrier = pltpu.get_barrier_semaphore()
    for peer in (
        (row, x_up), (row, x_down), (row, h_partner), (z_up, col), (z_down, col), (other_core, col)
    ):
        pl.semaphore_signal(barrier, inc=1, device_id=peer, device_id_type=MESH)
    for copy in first:
        copy.wait()
    pl.semaphore_wait(barrier, 6)

    def share(r, half):
        push("c", d_copy, r, half, other_core)

    def h_both(c):
        for n in range(2):
            h_wait(c, n)

    def d_both(r):
        for n in range(2):
            d_wait(r, n)

    def multiply(k, start, half=None):
        lines = slice(None) if half is None else slice(half * HALF, (half + 1) * HALF)

        def tile(n, carry):
            columns = pl.ds(pl.multiple_of(n * 256, 256), 256)
            part = jnp.dot(hbuf[k, lines], dbuf[k, :, columns], preferred_element_type=F32)
            if start:
                out[lines, columns] = part
            else:
                out[lines, columns] += part
            return carry

        lax.fori_loop(0, TILE_C // 256, tile, 0)

    for n in range(2):
        push("h", h_copy, col, n, x_up)
        push("h", h_copy, col, 1 - n, x_down)
        push("h", h_copy, col, n, h_partner)
    push("d", d_copy, d_partner, 0, z_up)
    push("d", d_copy, d_partner, 1, z_down)
    push("d", d_copy, z_down, 0, z_up)
    push("d", d_copy, z_up, 1, z_down)
    push("d", d_copy, d_partner, 1, z_up)
    push("d", d_copy, d_partner, 0, z_down)
    for r in (row, d_partner, z_down, z_up):
        for n in range(2):
            share(r, n)

    h_wait(x_down, 0)
    push("h", h_copy, x_down, 0, x_up)
    h_wait(x_up, 1)
    push("h", h_copy, x_up, 1, x_down)
    h_wait(h_partner, 0)
    push("h", h_copy, h_partner, 0, x_up)
    push("h", h_copy, h_partner, 0, x_down)
    d_wait(d_down, 0)
    push("d", d_copy, d_down, 0, z_up)
    d_wait(d_up, 1)
    push("d", d_copy, d_up, 1, z_down)
    share(d_down, 0)
    share(d_up, 1)
    h_wait(h_partner, 1)
    push("h", h_copy, h_partner, 1, x_up)
    push("h", h_copy, h_partner, 1, x_down)
    for n in range(2):
        far = row_of(ylo, z + 2, core)
        d_wait(far, n)
        share(far, n)
    d_wait(d_down, 1)
    share(d_down, 1)
    d_wait(d_up, 0)
    share(d_up, 0)
    h_wait(x_down, 1)
    h_wait(x_up, 0)
    for n in range(2):
        far = col_of(x + 2, yhi)
        h_wait(far, n)
        push("h", h_copy, far, n, h_partner)
    for n in range(4):
        d_both(row_of(ylo, z + n, 1 - core))
    multiply(ylo * 4 + yhi, True)
    multiply(ylo * 4 + 2 + yhi, False)
    for n in range(2):
        far = row_of(1 - ylo, z + 2, core)
        d_wait(far, n)
        share(far, n)
    for n in range(4):
        d_both(row_of(1 - ylo, z + n, 1 - core))
    multiply((1 - ylo) * 4 + yhi, False)
    multiply((1 - ylo) * 4 + 2 + yhi, False)
    multiply(h_partner, False)
    for half in range(2):
        for c in (h_down, h_up):
            h_wait(c, half)
            multiply(c, False, half)
    for half in range(2):
        far = col_of(x + 2, 1 - yhi)
        h_wait(far, half)
        multiply(far, False, half)
    for copy in sent:
        copy.wait_send()


def multiply_all(ham, den):
    return pl.pallas_call(
        product_kernel,
        name="product",
        out_shape=jax.ShapeDtypeStruct((TILE_R, TILE_C), F32),
        in_specs=[hbm(), hbm()],
        out_specs=vmem(),
        scratch_shapes=[
            pltpu.VMEM((COLS, TILE_R, TILE_C), BF16),
            pltpu.VMEM((COLS, 2 * TILE_R, TILE_C), BF16),
            pltpu.SemaphoreType.DMA((5,)),
            pltpu.SemaphoreType.DMA((16,)),
            pltpu.SemaphoreType.DMA((16,)),
            pltpu.SemaphoreType.DMA((16,)),
            pltpu.SemaphoreType.DMA((COLS, 2)),
            pltpu.SemaphoreType.DMA((ROWS, 2)),
        ],
        compiler_params=pltpu.CompilerParams(
            has_side_effects=True, vmem_limit_bytes=56 << 20, collective_id=1
        ),
    )(ham, den)


def shards(
    potential, basis_left, basis_right, core_matrix, density, pattern, pair_atoms, cube_offsets, live_count
):
    corner = jnp.stack([lax.axis_index("row") * ATOM_ROWS, lax.axis_index("col") * ATOM_COLS]).astype(I32)
    received, received_ids, near_den = exchange(
        cube_offsets.T, pair_atoms.T, live_count, pattern, potential.reshape(4, 64, 8, 512), density, basis_left, basis_right
    )
    ham = combine(pattern, corner, received_ids, received, core_matrix)
    return ham, multiply_all(ham, near_den)


def solution(mesh):
    flat = ("row", "col")
    tile = P("row", "col")
    placed = (
        P(flat, None, None),
        P(flat, None, None),
        P(flat, None, None),
        tile,
        tile,
        P(),
        P(flat, None),
        P(flat, None),
        P(flat),
    )
    return jax.shard_map(
        shards, mesh=mesh, in_specs=placed, out_specs=(tile, tile), check_vma=False
    )
```

time: 224 us -> 173 us (0.77)
  Pallas kernels: 203 us -> 165 us
  starting transfers between devices: 6.53 us -> 0 us
  waiting for transfers between devices: 5.76 us -> 0 us
    pallas_call x1, Pallas kernels: 108 us -> 67.7 us  [multiply_all(): pl.pallas_call(product_kernel, name='product', out_shape=jax.ShapeDtypeSt...]
    pallas_call x1, Pallas kernels: 71.1 us -> 90.5 us  [exchange(): pl.pallas_call(exchange_kernel, name='exchange', out_shape=(jax.ShapeDtyp...]
    pallas_call x1 -> x0, Pallas kernels: 17.5 us -> none  [cut_cubes(): pl.pallas_call(cube_kernel, name='cut_cubes', out_shape=(jax.ShapeDtypeSt...]
    ppermute x2 -> x0, starting transfers between devices: 6.53 us -> none  [the longest x1 6.53 us: shards(): lax.ppermute(cube_offsets, ('row', 'col'), [(b, a) for a, b in up])]
    ppermute x2 -> x0, waiting for transfers between devices: 5.76 us -> none  [the longest x1 5.76 us: shards(): left_off = lax.ppermute(cube_offsets, ('row', 'col'), up)]
  transfers between devices with their start and end apart: 2 -> 0, of which waited for: 1 -> 0; matrix products, arithmetic and copies ran while one was open for 0% -> 0% of each run, Pallas kernels for 0% -> 0%
where the time goes in v2:
time: 173 us
  Pallas kernels  165 us (95%)
  local copies, waits for them, and re-layouts  6.5 us (4%)
    pallas_call x1, Pallas kernels, exchange(): pl.pallas_call(exchange_kernel, name='exchange', out_shape=(jax.ShapeDtyp...  90.5 us
    pallas_call x1, Pallas kernels, multiply_all(): pl.pallas_call(product_kernel, name='product', out_shape=jax.ShapeDtypeSt...  67.7 us
    pallas_call x1, Pallas kernels, combine(): pl.pallas_call(combine_kernel, name='combine', out_shape=jax.ShapeDtypeSt...  6.61 us
    unnamed x11, local copies, waits for them, and re-layouts  6.5 us

profile of v2, /device:TPU:1, one launch (start us, length us, event | category | flops | bytes accessed | tf_op | source)
XLA Modules:
  0.0 172.7 jit_solution(8248418206380549075)
XLA Ops:
  1.3 0.1 pad_add_fusion.corner
  1.4 0.0 copy-start
  1.4 1.2 copy-done
  2.6 0.0 copy-start.2
  2.6 0.8 copy-done.2
  3.3 0.0 copy-start.3
  3.3 0.7 copy-done.3
  4.0 0.0 copy-start.4
  4.0 0.7 copy-done.4
  4.7 0.0 copy-start.1
  4.7 90.5 %exchange.1 = (bf16[128,128,128]{2,1,0:T(8,128)(2,1)S(1)}, s32[128,1,128]{2,1,0:T(1,128)S(1)}, bf16[4,512,1024]{2,1,0:T(8,128)(2,1)}) custom-call(s32[3,64]{1,0:T(4,128)S(1)} %bitcast.5, s32[2,64]{1,0:T(2,128)S(1)} %bitcast.6, s32[1]{0:T(128)S(6)} %copy.12.live, s32[64,64]{1,0:T(8,128)S(1)} %copy-done.2, f32[4,64,8,512]{3,2,1,0:T(8,128)} %bitcast.7, ...), custom_call_target="tpu_custom_call" | custom-call | tf_op jit(solution)/shard_map/exchange/pallas_call | solution.py:337
  95.2 0.0 copy-done.1
  95.2 6.6 %combine.1.ham = bf16[512,1024]{1,0:T(8,128)(2,1)} custom-call(s32[64,64]{1,0:T(8,128)S(1)} %copy-done.2, s32[2]{0:T(128)S(1)} %pad_add_fusion.corner, s32[128,1,128]{2,1,0:T(1,128)S(1)} %get-tuple-element.5.ids_hbm, bf16[128,128,128]{2,1,0:T(8,128)(2,1)S(1)} %get-tuple-element.6.received, bf16[512,1024]{1,0:T(8,128)(2,1)S(1)} %copy-done.1), custom_call_target="tpu_custom_call" | custom-call | tf_op jit(solution)/shard_map/combine/pallas_call | solution.py:405
  101.9 67.7 %product.1 = f32[512,1024]{1,0:T(8,128)} custom-call(bf16[512,1024]{1,0:T(8,128)(2,1)} %combine.1.ham, bf16[4,512,1024]{2,1,0:T(8,128)(2,1)} %get-tuple-element.7.den), custom_call_target="tpu_custom_call" | custom-call | tf_op jit(solution)/shard_map/product/pallas_call | solution.py:591
  169.6 3.2 %copy.13 = f32[512,1024]{1,0:T(8,128)} copy(f32[512,1024]{1,0:T(8,128)} %product.1) | data formatting | bytes 4194304
Async XLA Ops:
  1.4 1.2 copy-start
  2.6 0.8 copy-start.2
  3.3 0.7 copy-start.3
  4.0 0.7 copy-start.4
  4.7 90.5 %copy-start.1 = (bf16[512,1024]{1,0:T(8,128)(2,1)S(1)}, bf16[512,1024]{1,0:T(8,128)(2,1)}, u32[]{:S(2)}) copy-start(bf16[512,1024]{1,0:T(8,128)(2,1)} %core.1) | copy-start | bytes 3145732

commit v3 on v2

--- a/solution.py
+++ b/solution.py
@@ -21,7 +21,6 @@
 TILE_C = 1024
 HALF = 256
 STRIDE = 51
-SPLIT = 40
 MESH = pl.DeviceIdType.MESH
 F32 = jnp.float32
 BF16 = jnp.bfloat16
@@ -40,17 +39,21 @@
     return pl.BlockSpec(memory_space=pl.ANY)
 
 
+def far_hbm():
+    return pl.BlockSpec(memory_space=pltpu.HBM)
+
+
 def place_of(index):
     return (index // COLS, index % COLS)
 
 
 def exchange_kernel(
-    offsets, pairs, live, pattern, pot, density, left, right,
-    received, received_ids, near_den,
-    pot_v, den_v, left_v, right_v, windows, own_off, other_off, off_s, table, table_s, ids,
+    offsets_h, pairs_h, live, pattern_h, pot, density, left, right,
+    received, info, near_den,
+    offsets, pairs, pattern, received_ids, pot_v, den_v, left_v, right_v, windows, own_off, other_off, off_s, table, table_s, ids,
     to_right, to_left, low, high, cubes, blocks,
     load_sem, off_send, off_recv, copy_sem, near_send, near_recv, send, recv, id_send, id_recv,
-    den_send, den_recv, local,
+    den_send, den_recv, local, small_sem, entered,
 ):
     row = lax.axis_index("row")
     col = lax.axis_index("col")
@@ -68,18 +71,32 @@
         )
         for n in range(4)
     ]
-    for copy in loads[:1] + pot_loads + loads[1:]:
+    small = [
+        pltpu.make_async_copy(a, b, small_sem.at[n])
+        for n, (a, b) in enumerate(((offsets_h, offsets), (pairs_h, pairs), (pattern_h, pattern)))
+    ]
+    for copy in small + loads[:1] + pot_loads + loads[1:]:
         copy.start()
     barrier = pltpu.get_barrier_semaphore()
 
-    def greet(k, carry):
-        pl.semaphore_signal(
-            barrier, inc=1, device_id=place_of((me + k) % DEVICES), device_id_type=MESH
-        )
-        return carry
-
-    lax.fori_loop(1, DEVICES, greet, 0)
-
+    def greet(device):
+        pl.semaphore_signal(barrier, inc=1, device_id=device, device_id_type=MESH)
+
+    def greet_row(k, carry):
+        greet((row, (col + k) % COLS))
+        return carry
+
+    def greet_col(k, carry):
+        greet(((row + k) % ROWS, col))
+        return carry
+
+    greet(above)
+    greet(below)
+    lax.fori_loop(1, COLS, greet_row, 0)
+    lax.fori_loop(1, ROWS, greet_col, 0)
+
+    for copy in small:
+        copy.wait()
     own_off[...] = jnp.zeros((8, 128), I32)
     own_off[0:1, 0:ENTRIES] = offsets[0:1, :]
     own_y = offsets[1:2, :]
@@ -119,11 +136,35 @@
     table_scalars.start()
 
     loads[0].wait()
+    pick_rows = (
+        lax.broadcasted_iota(I32, (8, NATOMS), 1)
+        == row * ATOM_ROWS + lax.broadcasted_iota(I32, (8, NATOMS), 0)
+    )
+    pick_cols = (
+        lax.broadcasted_iota(I32, (NATOMS, TILE_C), 0)
+        == col * ATOM_COLS + lax.broadcasted_iota(I32, (NATOMS, TILE_C), 1) // NB
+    )
+    pick_again = (
+        lax.broadcasted_iota(I32, (NATOMS, 128), 0)
+        == col * ATOM_COLS + lax.broadcasted_iota(I32, (NATOMS, 128), 1) % ATOM_COLS
+    )
+
+    def flags(chosen):
+        return jnp.where(chosen, 1.0, 0.0).astype(BF16)
+
+    on_rows = jnp.dot(flags(pick_rows), flags(pattern[...] > 0), preferred_element_type=F32).astype(BF16)
+    on_wide = jnp.dot(on_rows, flags(pick_cols), preferred_element_type=F32)
+    on_again = jnp.dot(on_rows, flags(pick_again), preferred_element_type=F32)
+    mine = (
+        lax.broadcasted_iota(I32, (8, 128), 1) // ATOM_COLS == lax.broadcasted_iota(I32, (8, 128), 0)
+    )
+    info[...] = jnp.zeros((8, 128), I32)
+    info[1:2, :] = jnp.sum(
+        jnp.where(jnp.logical_and(mine, on_again > 0.0), 1, 0), axis=0, keepdims=True
+    )
     for i in range(ATOM_ROWS):
-        for j in range(ATOM_COLS):
-            on = jnp.full((NB, NB), pattern[row * ATOM_ROWS + i, col * ATOM_COLS + j], I32) > 0
-            box = (slice(i * NB, (i + 1) * NB), slice(j * NB, (j + 1) * NB))
-            den_v[box] = jnp.where(on, den_v[box].astype(F32), 0.0).astype(BF16)
+        lines = slice(i * NB, (i + 1) * NB)
+        den_v[lines] = jnp.where(on_wide[i : i + 1, :] > 0.0, den_v[lines].astype(F32), 0.0).astype(BF16)
     keep_den = pltpu.make_async_copy(den_v, near_den.at[0], local.at[2])
     keep_den.start()
 
@@ -158,7 +199,7 @@
             cut(2, e * 4 + n, ((3, 0),))
         return carry
 
-    pl.semaphore_wait(barrier, DEVICES - 1)
+    pl.semaphore_wait(barrier, ROWS + COLS)
     off_copies = (
         pltpu.make_async_remote_copy(
             own_off, other_off.at[0], off_send.at[0], off_recv.at[0], below, MESH
@@ -170,6 +211,14 @@
     for copy in off_copies:
         copy.start()
 
+    def tell(k, carry):
+        pl.semaphore_signal(
+            entered, inc=1, device_id=(row, (col + k) % COLS), device_id_type=MESH
+        )
+        return carry
+
+    lax.fori_loop(1, COLS, tell, 0)
+
     def den_copy(slot, half, device):
         part = pl.ds(half * HALF, HALF)
         return pltpu.make_async_remote_copy(
@@ -179,13 +228,14 @@
 
     z = row // 2 % 4
     base = row - z * 2
-    den_targets = (
-        (1, ((row + 8) % ROWS, col)),
-        (2, (base + (z + 1) % 4 * 2, col)),
-        (3, (base + (z + 3) % 4 * 2, col)),
-    )
-    den_copies = [[den_copy(slot, half, device) for slot, device in den_targets] for half in range(2)]
-    for copy in den_copies[0]:
+    d_partner = ((row + 8) % ROWS, col)
+    den_copies = (
+        den_copy(1, 0, d_partner),
+        den_copy(2, 0, (base + (z + 1) % 4 * 2, col)),
+        den_copy(3, 1, (base + (z + 3) % 4 * 2, col)),
+        den_copy(1, 1, d_partner),
+    )
+    for copy in den_copies[:3]:
         copy.start()
 
     own_scalars.wait()
@@ -244,8 +294,10 @@
         copy.start()
     table_scalars.wait()
 
+    own_lane = lax.broadcasted_iota(I32, (1, 128), 1) == me
+
     def write_id(d, carry):
-        ids[d] = jnp.full((1, 128), table_s[1, d], I32)
+        ids[d] = jnp.where(own_lane, jnp.full((1, 128), table_s[1, d] + 1, I32), 0)
         return carry
 
     lax.fori_loop(0, DEVICES, write_id, 0)
@@ -275,6 +327,8 @@
         id_copy((me + k) % DEVICES).start()
         return carry
 
+    pl.semaphore_wait(entered, COLS - 1)
+    den_copies[3].start()
     lax.fori_loop(1, DEVICES, send_id, 0)
     own_id = pltpu.make_async_copy(ids.at[me], received_ids.at[me], local.at[0])
     own_id.start()
@@ -307,10 +361,7 @@
         block_copy(target_at(k - 1)).start()
         return carry
 
-    lax.fori_loop(2, SPLIT, step, 0)
-    for copy in den_copies[1]:
-        copy.start()
-    lax.fori_loop(SPLIT, DEVICES, step, 0)
+    lax.fori_loop(2, DEVICES, step, 0)
     make(me)
     block_copy(target_at(DEVICES - 1)).start()
     own_block = pltpu.make_async_copy(blocks.at[me], received.at[me], local.at[1])
@@ -326,9 +377,9 @@
         blocks.at[all_but_one], received.at[all_but_one], send, recv, above, MESH
     )
     ids_done.wait()
-    for half in range(2):
-        for copy in den_copies[half]:
-            copy.wait()
+    info[0:1, :] = jnp.sum(received_ids[...], axis=0) - 1
+    for copy in den_copies:
+        copy.wait()
     blocks_done.wait()
 
 
@@ -339,12 +390,16 @@
         name="exchange",
         out_shape=(
             jax.ShapeDtypeStruct((DEVICES, NB, NB), BF16),
-            jax.ShapeDtypeStruct((DEVICES, 1, 128), I32),
+            jax.ShapeDtypeStruct((8, 128), I32),
             jax.ShapeDtypeStruct((4, TILE_R, TILE_C), BF16),
         ),
-        in_specs=[vmem(), vmem(), smem(), smem()] + [hbm()] * 4,
-        out_specs=(hbm(), hbm(), hbm()),
+        in_specs=[far_hbm(), far_hbm(), smem()] + [far_hbm()] * 5,
+        out_specs=(hbm(), vmem(), hbm()),
         scratch_shapes=[
+            pltpu.VMEM((3, ENTRIES), I32),
+            pltpu.VMEM((2, ENTRIES), I32),
+            pltpu.VMEM((NATOMS, NATOMS), I32),
+            pltpu.VMEM((DEVICES, 1, 128), I32),
             pltpu.VMEM((4, 4, 64, 8, 128), F32),
             pltpu.VMEM((TILE_R, TILE_C), BF16),
             pltpu.VMEM((ENTRIES, NB, CELLS), BF16),
@@ -364,6 +419,7 @@
             pltpu.VMEM((DEVICES, NB, NB), BF16),
             dma((7,)), dma((2,)), dma((2,)), dma((4,)), dma((2,)), dma((2,)),
             dma, dma, dma, dma, dma((4, 2)), dma((4, 2)), dma((3,)),
+            dma((3,)), pltpu.SemaphoreType.REGULAR,
         ],
         compiler_params=pltpu.CompilerParams(
             has_side_effects=True, vmem_limit_bytes=48 << 20, collective_id=0
@@ -371,50 +427,57 @@
     )(offsets, pairs, live, pattern, pot, density, left, right)
 
 
-def combine_kernel(pattern, corner, ids_hbm, received, core, ham, total, ids, sem):
-    copy = pltpu.make_async_copy(ids_hbm, ids, sem)
-    copy.start()
-    total[...] = jnp.zeros(total.shape, F32)
-    copy.wait()
-
-    def add(s, carry):
-        slot = ids[s, 0, 0]
+def combine_kernel(info, received, core, ham, head, after):
+    def clear(b, carry):
+        head[b] = -1
+        return carry
+
+    lax.fori_loop(0, LOCAL, clear, 0)
+
+    def link(s, carry):
+        slot = info[0, s]
 
         @pl.when(slot >= 0)
         def _():
-            total[slot] += received[s].astype(F32)
-
-        return carry
-
-    lax.fori_loop(0, DEVICES, add, 0)
+            after[s] = head[slot]
+            head[slot] = s
+
+        return carry
+
+    lax.fori_loop(0, DEVICES, link, 0)
+
+    def more(state):
+        s, total = state
+        return after[s], total + received[s].astype(F32)
+
     for i in range(ATOM_ROWS):
         for j in range(ATOM_COLS):
-            on = pattern[corner[0] + i, corner[1] + j] > 0
+            block = i * ATOM_COLS + j
             box = (slice(i * NB, (i + 1) * NB), slice(j * NB, (j + 1) * NB))
+            on = info[1, block] > 0
 
             @pl.when(on)
             def _():
-                ham[box] = (core[box].astype(F32) + total[i * ATOM_COLS + j]).astype(BF16)
+                total = lax.while_loop(
+                    lambda state: state[0] >= 0, more, (head[block], core[box].astype(F32))
+                )[1]
+                ham[box] = total.astype(BF16)
 
             @pl.when(jnp.logical_not(on))
             def _():
                 ham[box] = jnp.zeros((NB, NB), BF16)
 
 
-def combine(pattern, corner, ids, received, core):
+def combine(info, received, core):
     return pl.pallas_call(
         combine_kernel,
         name="combine",
         out_shape=jax.ShapeDtypeStruct((TILE_R, TILE_C), BF16),
-        in_specs=[smem(), smem(), hbm(), vmem(), vmem()],
+        in_specs=[smem(), vmem(), vmem()],
         out_specs=vmem(),
-        scratch_shapes=[
-            pltpu.VMEM((LOCAL, NB, NB), F32),
-            pltpu.SMEM((DEVICES, 1, 128), I32),
-            pltpu.SemaphoreType.DMA,
-        ],
+        scratch_shapes=[pltpu.SMEM((LOCAL,), I32), pltpu.SMEM((DEVICES,), I32)],
         compiler_params=pltpu.CompilerParams(vmem_limit_bytes=48 << 20),
-    )(pattern, corner, ids, received, core)
+    )(info, received, core)
 
 
 def product_kernel(ham, den, out, hbuf, dbuf, load, hsend, dsend, csend, hrecv, drecv):
@@ -476,11 +539,11 @@
 
     first = [pltpu.make_async_copy(ham, hbuf.at[col], load.at[0])] + [
         pltpu.make_async_copy(
-            den.at[n],
-            dbuf.at[r // 2, pl.ds(pl.multiple_of(core * TILE_R, TILE_R), TILE_R), :],
-            load.at[n + 1],
-        )
-        for n, r in enumerate((row, d_partner, z_down, z_up))
+            den.at[slot, pl.ds(half * HALF, HALF), :], d_at(r, half), load.at[n + 1]
+        )
+        for n, (slot, r, half) in enumerate(
+            ((0, row, 0), (0, row, 1), (1, d_partner, 0), (1, d_partner, 1), (2, z_down, 0), (3, z_up, 1))
+        )
     ]
     for copy in first:
         copy.start()
@@ -505,7 +568,10 @@
             d_wait(r, n)
 
     def multiply(k, start, half=None):
-        lines = slice(None) if half is None else slice(half * HALF, (half + 1) * HALF)
+        if half is None:
+            lines = slice(None)
+        else:
+            lines = pl.ds(pl.multiple_of(half * HALF, HALF), HALF)
 
         def tile(n, carry):
             columns = pl.ds(pl.multiple_of(n * 256, 256), 256)
@@ -522,15 +588,16 @@
         push("h", h_copy, col, n, x_up)
         push("h", h_copy, col, 1 - n, x_down)
         push("h", h_copy, col, n, h_partner)
+    push("d", d_copy, row, 1, z_up)
+    push("d", d_copy, row, 0, z_down)
     push("d", d_copy, d_partner, 0, z_up)
     push("d", d_copy, d_partner, 1, z_down)
     push("d", d_copy, z_down, 0, z_up)
     push("d", d_copy, z_up, 1, z_down)
     push("d", d_copy, d_partner, 1, z_up)
     push("d", d_copy, d_partner, 0, z_down)
-    for r in (row, d_partner, z_down, z_up):
-        for n in range(2):
-            share(r, n)
+    for r, half in ((row, 0), (row, 1), (d_partner, 0), (d_partner, 1), (z_down, 0), (z_up, 1)):
+        share(r, half)
 
     h_wait(x_down, 0)
     push("h", h_copy, x_down, 0, x_up)
@@ -539,6 +606,10 @@
     h_wait(h_partner, 0)
     push("h", h_copy, h_partner, 0, x_up)
     push("h", h_copy, h_partner, 0, x_down)
+    d_wait(z_down, 1)
+    share(z_down, 1)
+    d_wait(z_up, 0)
+    share(z_up, 0)
     d_wait(d_down, 0)
     push("d", d_copy, d_down, 0, z_up)
     d_wait(d_up, 1)
@@ -548,16 +619,12 @@
     h_wait(h_partner, 1)
     push("h", h_copy, h_partner, 1, x_up)
     push("h", h_copy, h_partner, 1, x_down)
+    h_wait(x_down, 1)
+    h_wait(x_up, 0)
     for n in range(2):
         far = row_of(ylo, z + 2, core)
         d_wait(far, n)
         share(far, n)
-    d_wait(d_down, 1)
-    share(d_down, 1)
-    d_wait(d_up, 0)
-    share(d_up, 0)
-    h_wait(x_down, 1)
-    h_wait(x_up, 0)
     for n in range(2):
         far = col_of(x + 2, yhi)
         h_wait(far, n)
@@ -566,23 +633,45 @@
         d_both(row_of(ylo, z + n, 1 - core))
     multiply(ylo * 4 + yhi, True)
     multiply(ylo * 4 + 2 + yhi, False)
-    for n in range(2):
+    d_wait(d_down, 1)
+    share(d_down, 1)
+    d_wait(d_up, 0)
+    share(d_up, 0)
+    for n in (0, 1, 3):
+        d_both(row_of(1 - ylo, z + n, 1 - core))
+
+    h_far = col_of(x + 2, 1 - yhi)
+    late = (1 - ylo) * 4 + (z + 2) % 4
+    ready = (1 - ylo) * 4 + yhi
+    units = [(k, half) for k in (ready, ready + 2, h_partner) for half in range(2)]
+    units += [(k, half) for half in range(2) for k in (h_down, h_up)]
+    units += [(h_far, half) for half in range(2)]
+    passed = 0
+    spots = []
+    for k, half in units:
+        is_late = jnp.where(k == late, 1, 0)
+        spots.append((is_late, len(spots) - passed))
+        passed = passed + is_late
+
+    def d_late(n):
         far = row_of(1 - ylo, z + 2, core)
         d_wait(far, n)
         share(far, n)
-    for n in range(4):
-        d_both(row_of(1 - ylo, z + n, 1 - core))
-    multiply((1 - ylo) * 4 + yhi, False)
-    multiply((1 - ylo) * 4 + 2 + yhi, False)
-    multiply(h_partner, False)
-    for half in range(2):
-        for c in (h_down, h_up):
-            h_wait(c, half)
-            multiply(c, False, half)
-    for half in range(2):
-        far = col_of(x + 2, 1 - yhi)
-        h_wait(far, half)
-        multiply(far, False, half)
+
+    for spot in range(len(units) - 2):
+        if 6 <= spot + 2:
+            h_wait(*units[spot + 2])
+        if spot in (6, 7):
+            d_late(spot - 6)
+        k = 0
+        half = 0
+        for (unit_k, unit_half), (is_late, at) in zip(units, spots):
+            here = jnp.where(at == spot, 1 - is_late, 0)
+            k = k + here * unit_k
+            half = half + here * unit_half
+        multiply(k, False, half)
+    d_both(row_of(1 - ylo, z + 2, 1 - core))
+    multiply(late, False)
     for copy in sent:
         copy.wait_send()
 
@@ -597,7 +686,7 @@
         scratch_shapes=[
             pltpu.VMEM((COLS, TILE_R, TILE_C), BF16),
             pltpu.VMEM((COLS, 2 * TILE_R, TILE_C), BF16),
-            pltpu.SemaphoreType.DMA((5,)),
+            pltpu.SemaphoreType.DMA((7,)),
             pltpu.SemaphoreType.DMA((16,)),
             pltpu.SemaphoreType.DMA((16,)),
             pltpu.SemaphoreType.DMA((16,)),
@@ -605,7 +694,7 @@
             pltpu.SemaphoreType.DMA((ROWS, 2)),
         ],
         compiler_params=pltpu.CompilerParams(
-            has_side_effects=True, vmem_limit_bytes=56 << 20, collective_id=1
+            has_side_effects=True, vmem_limit_bytes=40 << 20, collective_id=1
         ),
     )(ham, den)
 
@@ -613,11 +702,11 @@
 def shards(
     potential, basis_left, basis_right, core_matrix, density, pattern, pair_atoms, cube_offsets, live_count
 ):
-    corner = jnp.stack([lax.axis_index("row") * ATOM_ROWS, lax.axis_index("col") * ATOM_COLS]).astype(I32)
-    received, received_ids, near_den = exchange(
-        cube_offsets.T, pair_atoms.T, live_count, pattern, potential.reshape(4, 64, 8, 512), density, basis_left, basis_right
-    )
-    ham = combine(pattern, corner, received_ids, received, core_matrix)
+    received, info, near_den = exchange(
+        cube_offsets.T, pair_atoms.T, live_count, pattern, potential.reshape(4, 64, 8, 512),
+        density, basis_left, basis_right,
+    )
+    ham = combine(info, received, core_matrix)
     return ham, multiply_all(ham, near_den)
 
 

time: 173 us -> 161 us (0.931)
  Pallas kernels: 165 us -> 154 us
    pallas_call x1, Pallas kernels: 90.5 us -> 80.4 us  [exchange(): pl.pallas_call(exchange_kernel, name='exchange', out_shape=(jax.ShapeDtyp...]
    pallas_call x1, Pallas kernels: 6.61 us -> 4.45 us  [combine(): pl.pallas_call(combine_kernel, name='combine', out_shape=jax.ShapeDtypeSt...]
    unnamed x11 -> x15, local copies, waits for them, and re-layouts: 6.5 us -> 5.89 us
where the time goes in v3:
time: 161 us
  Pallas kernels  154 us (96%)
  local copies, waits for them, and re-layouts  5.89 us (4%)
    pallas_call x1, Pallas kernels, exchange(): pl.pallas_call(exchange_kernel, name='exchange', out_shape=(jax.ShapeDtyp...  80.4 us
    pallas_call x1, Pallas kernels, multiply_all(): pl.pallas_call(product_kernel, name='product', out_shape=jax.ShapeDtypeSt...  68.7 us
    unnamed x15, local copies, waits for them, and re-layouts  5.89 us
    pallas_call x1, Pallas kernels, combine(): pl.pallas_call(combine_kernel, name='combine', out_shape=jax.ShapeDtypeSt...  4.45 us

profile of v3, /device:TPU:1, one launch (start us, length us, event | category | flops | bytes accessed | tf_op | source)
XLA Modules:
  0.0 160.7 jit_solution(16460905064674778763)
XLA Ops:
  1.3 0.0 copy-start.2
  1.3 1.2 copy-done.2
  2.5 0.0 copy-start.4
  2.5 0.8 copy-done.4
  3.3 0.0 copy-start.5
  3.3 0.7 copy-done.5
  3.9 0.0 copy-start.6
  3.9 0.7 copy-done.6
  4.6 0.0 copy-start.3
  4.6 80.4 %exchange.1 = (bf16[128,128,128]{2,1,0:T(8,128)(2,1)S(1)}, s32[8,128]{1,0:T(8,128)S(1)}, bf16[4,512,1024]{2,1,0:T(8,128)(2,1)}) custom-call(s32[3,64]{1,0:T(4,128)S(1)} %bitcast.3, s32[2,64]{1,0:T(2,128)S(1)} %bitcast.4, s32[1]{0:T(128)S(6)} %copy.12.live, s32[64,64]{1,0:T(8,128)S(1)} %copy-done.4, f32[4,64,8,512]{3,2,1,0:T(8,128)} %bitcast.5, ...), custom_call_target="tpu_custom_call" | custom-call | tf_op jit(solution)/shard_map/exchange/pallas_call | solution.py:388
  85.0 0.0 copy-start
  85.0 0.0 copy-done.3
  85.0 4.5 %combine.1.ham = bf16[512,1024]{1,0:T(8,128)(2,1)} custom-call(s32[8,128]{1,0:T(8,128)S(1)} %get-tuple-element.5.info, bf16[128,128,128]{2,1,0:T(8,128)(2,1)S(1)} %get-tuple-element.6.received, bf16[512,1024]{1,0:T(8,128)(2,1)S(1)} %copy-done.3), custom_call_target="tpu_custom_call" | custom-call | tf_op jit(solution)/shard_map/combine/pallas_call | solution.py:472
  89.5 0.0 copy-done
  89.5 0.0 copy-start.1
  89.5 1.2 copy-done.1
  90.7 68.7 %product.1 = f32[512,1024]{1,0:T(8,128)S(1)} custom-call(bf16[512,1024]{1,0:T(8,128)(2,1)S(1)} %copy-done.1, bf16[4,512,1024]{2,1,0:T(8,128)(2,1)S(1)} %copy-done), custom_call_target="tpu_custom_call" | custom-call | tf_op jit(solution)/shard_map/product/pallas_call | solution.py:680
  159.4 1.3 copy.13
Async XLA Ops:
  1.3 1.2 copy-start.2
  2.5 0.8 copy-start.4
  3.3 0.7 copy-start.5
  3.9 0.7 copy-start.6
  4.6 80.4 %copy-start.3 = (bf16[512,1024]{1,0:T(8,128)(2,1)S(1)}, bf16[512,1024]{1,0:T(8,128)(2,1)}, u32[]{:S(2)}) copy-start(bf16[512,1024]{1,0:T(8,128)(2,1)} %core.1) | copy-start | bytes 3145732
  85.0 4.5 %copy-start = (bf16[4,512,1024]{2,1,0:T(8,128)(2,1)S(1)}, bf16[4,512,1024]{2,1,0:T(8,128)(2,1)}, u32[]{:S(2)}) copy-start(bf16[4,512,1024]{2,1,0:T(8,128)(2,1)} %get-tuple-element.7.den) | copy-start | bytes 12582916
  89.5 1.2 copy-start.1

commit v4 on v3

--- a/solution.py
+++ b/solution.py
@@ -135,39 +135,6 @@
     table_scalars = pltpu.make_async_copy(table, table_s, copy_sem.at[1])
     table_scalars.start()
 
-    loads[0].wait()
-    pick_rows = (
-        lax.broadcasted_iota(I32, (8, NATOMS), 1)
-        == row * ATOM_ROWS + lax.broadcasted_iota(I32, (8, NATOMS), 0)
-    )
-    pick_cols = (
-        lax.broadcasted_iota(I32, (NATOMS, TILE_C), 0)
-        == col * ATOM_COLS + lax.broadcasted_iota(I32, (NATOMS, TILE_C), 1) // NB
-    )
-    pick_again = (
-        lax.broadcasted_iota(I32, (NATOMS, 128), 0)
-        == col * ATOM_COLS + lax.broadcasted_iota(I32, (NATOMS, 128), 1) % ATOM_COLS
-    )
-
-    def flags(chosen):
-        return jnp.where(chosen, 1.0, 0.0).astype(BF16)
-
-    on_rows = jnp.dot(flags(pick_rows), flags(pattern[...] > 0), preferred_element_type=F32).astype(BF16)
-    on_wide = jnp.dot(on_rows, flags(pick_cols), preferred_element_type=F32)
-    on_again = jnp.dot(on_rows, flags(pick_again), preferred_element_type=F32)
-    mine = (
-        lax.broadcasted_iota(I32, (8, 128), 1) // ATOM_COLS == lax.broadcasted_iota(I32, (8, 128), 0)
-    )
-    info[...] = jnp.zeros((8, 128), I32)
-    info[1:2, :] = jnp.sum(
-        jnp.where(jnp.logical_and(mine, on_again > 0.0), 1, 0), axis=0, keepdims=True
-    )
-    for i in range(ATOM_ROWS):
-        lines = slice(i * NB, (i + 1) * NB)
-        den_v[lines] = jnp.where(on_wide[i : i + 1, :] > 0.0, den_v[lines].astype(F32), 0.0).astype(BF16)
-    keep_den = pltpu.make_async_copy(den_v, near_den.at[0], local.at[2])
-    keep_den.start()
-
     lane = lax.broadcasted_iota(I32, (8, 128), 1)
     line = lax.broadcasted_iota(I32, (8, 128), 0)
 
@@ -233,9 +200,41 @@
         den_copy(1, 0, d_partner),
         den_copy(2, 0, (base + (z + 1) % 4 * 2, col)),
         den_copy(3, 1, (base + (z + 3) % 4 * 2, col)),
-        den_copy(1, 1, d_partner),
-    )
-    for copy in den_copies[:3]:
+    )
+    loads[0].wait()
+    pick_rows = (
+        lax.broadcasted_iota(I32, (8, NATOMS), 1)
+        == row * ATOM_ROWS + lax.broadcasted_iota(I32, (8, NATOMS), 0)
+    )
+    pick_cols = (
+        lax.broadcasted_iota(I32, (NATOMS, TILE_C), 0)
+        == col * ATOM_COLS + lax.broadcasted_iota(I32, (NATOMS, TILE_C), 1) // NB
+    )
+    pick_again = (
+        lax.broadcasted_iota(I32, (NATOMS, 128), 0)
+        == col * ATOM_COLS + lax.broadcasted_iota(I32, (NATOMS, 128), 1) % ATOM_COLS
+    )
+
+    def flags(chosen):
+        return jnp.where(chosen, 1.0, 0.0).astype(BF16)
+
+    on_rows = jnp.dot(flags(pick_rows), flags(pattern[...] > 0), preferred_element_type=F32).astype(BF16)
+    on_wide = jnp.dot(on_rows, flags(pick_cols), preferred_element_type=F32)
+    on_again = jnp.dot(on_rows, flags(pick_again), preferred_element_type=F32)
+    mine = (
+        lax.broadcasted_iota(I32, (8, 128), 1) // ATOM_COLS == lax.broadcasted_iota(I32, (8, 128), 0)
+    )
+    info[...] = jnp.zeros((8, 128), I32)
+    info[1:2, :] = jnp.sum(
+        jnp.where(jnp.logical_and(mine, on_again > 0.0), 1, 0), axis=0, keepdims=True
+    )
+    for i in range(ATOM_ROWS):
+        lines = slice(i * NB, (i + 1) * NB)
+        den_v[lines] = jnp.where(on_wide[i : i + 1, :] > 0.0, den_v[lines].astype(F32), 0.0).astype(BF16)
+    keep_den = pltpu.make_async_copy(den_v, near_den.at[0], local.at[2])
+    keep_den.start()
+
+    for copy in den_copies:
         copy.start()
 
     own_scalars.wait()
@@ -284,7 +283,6 @@
             made.append(piece)
         return made
 
-    own_piece = pieces((0, 1), own_off[5:7, 0:ENTRIES])
     for copy in off_copies:
         copy.wait()
     other_scalars = [
@@ -312,6 +310,7 @@
     )
     for copy in near:
         copy.start()
+    own_piece = pieces((0, 1), own_off[5:7, 0:ENTRIES])
 
     def id_copy(target):
         return pltpu.make_async_remote_copy(
@@ -323,13 +322,7 @@
             blocks.at[target], received.at[me], send, recv, place_of(target), MESH
         )
 
-    def send_id(k, carry):
-        id_copy((me + k) % DEVICES).start()
-        return carry
-
     pl.semaphore_wait(entered, COLS - 1)
-    den_copies[3].start()
-    lax.fori_loop(1, DEVICES, send_id, 0)
     own_id = pltpu.make_async_copy(ids.at[me], received_ids.at[me], local.at[0])
     own_id.start()
     for copy in near:
@@ -359,11 +352,13 @@
     def step(k, carry):
         make(target_at(k))
         block_copy(target_at(k - 1)).start()
+        id_copy(target_at(k - 1)).start()
         return carry
 
     lax.fori_loop(2, DEVICES, step, 0)
+    block_copy(target_at(DEVICES - 1)).start()
+    id_copy(target_at(DEVICES - 1)).start()
     make(me)
-    block_copy(target_at(DEVICES - 1)).start()
     own_block = pltpu.make_async_copy(blocks.at[me], received.at[me], local.at[1])
     own_block.start()
     own_id.wait()
@@ -542,19 +537,20 @@
             den.at[slot, pl.ds(half * HALF, HALF), :], d_at(r, half), load.at[n + 1]
         )
         for n, (slot, r, half) in enumerate(
-            ((0, row, 0), (0, row, 1), (1, d_partner, 0), (1, d_partner, 1), (2, z_down, 0), (3, z_up, 1))
+            ((0, row, 0), (0, row, 1), (1, d_partner, 0), (2, z_down, 0), (3, z_up, 1))
         )
     ]
     for copy in first:
         copy.start()
     barrier = pltpu.get_barrier_semaphore()
     for peer in (
-        (row, x_up), (row, x_down), (row, h_partner), (z_up, col), (z_down, col), (other_core, col)
+        (row, x_up), (row, x_down), (row, h_partner),
+        (z_up, col), (z_down, col), (d_partner, col), (other_core, col),
     ):
         pl.semaphore_signal(barrier, inc=1, device_id=peer, device_id_type=MESH)
     for copy in first:
         copy.wait()
-    pl.semaphore_wait(barrier, 6)
+    pl.semaphore_wait(barrier, 7)
 
     def share(r, half):
         push("c", d_copy, r, half, other_core)
@@ -584,6 +580,7 @@
 
         lax.fori_loop(0, TILE_C // 256, tile, 0)
 
+    push("d", d_copy, row, 1, d_partner)
     for n in range(2):
         push("h", h_copy, col, n, x_up)
         push("h", h_copy, col, 1 - n, x_down)
@@ -591,18 +588,20 @@
     push("d", d_copy, row, 1, z_up)
     push("d", d_copy, row, 0, z_down)
     push("d", d_copy, d_partner, 0, z_up)
-    push("d", d_copy, d_partner, 1, z_down)
+    push("d", d_copy, z_up, 1, z_down)
     push("d", d_copy, z_down, 0, z_up)
-    push("d", d_copy, z_up, 1, z_down)
-    push("d", d_copy, d_partner, 1, z_up)
-    push("d", d_copy, d_partner, 0, z_down)
-    for r, half in ((row, 0), (row, 1), (d_partner, 0), (d_partner, 1), (z_down, 0), (z_up, 1)):
+    for r, half in ((row, 0), (row, 1), (d_partner, 0), (z_down, 0), (z_up, 1)):
         share(r, half)
 
     h_wait(x_down, 0)
     push("h", h_copy, x_down, 0, x_up)
     h_wait(x_up, 1)
     push("h", h_copy, x_up, 1, x_down)
+    d_wait(d_partner, 1)
+    push("d", d_copy, d_partner, 1, z_down)
+    push("d", d_copy, d_partner, 1, z_up)
+    push("d", d_copy, d_partner, 0, z_down)
+    share(d_partner, 1)
     h_wait(h_partner, 0)
     push("h", h_copy, h_partner, 0, x_up)
     push("h", h_copy, h_partner, 0, x_down)

time: 161 us -> 155 us (0.963)
  Pallas kernels: 154 us -> 147 us
    pallas_call x1, Pallas kernels: 80.4 us -> 74.2 us  [exchange(): pl.pallas_call(exchange_kernel, name='exchange', out_shape=(jax.ShapeDtyp...]
where the time goes in v4:
time: 155 us
  Pallas kernels  147 us (95%)
  local copies, waits for them, and re-layouts  5.89 us (4%)
    pallas_call x1, Pallas kernels, exchange(): pl.pallas_call(exchange_kernel, name='exchange', out_shape=(jax.ShapeDtyp...  74.2 us
    pallas_call x1, Pallas kernels, multiply_all(): pl.pallas_call(product_kernel, name='product', out_shape=jax.ShapeDtypeSt...  68.7 us
    unnamed x15, local copies, waits for them, and re-layouts  5.89 us
    pallas_call x1, Pallas kernels, combine(): pl.pallas_call(combine_kernel, name='combine', out_shape=jax.ShapeDtypeSt...  4.35 us

profile of v4, /device:TPU:1, one launch (start us, length us, event | category | flops | bytes accessed | tf_op | source)
XLA Modules:
  0.0 154.6 jit_solution(1265482128293880448)
XLA Ops:
  1.3 0.0 copy-start.2
  1.3 1.2 copy-done.2
  2.5 0.0 copy-start.4
  2.5 0.8 copy-done.4
  3.3 0.0 copy-start.5
  3.3 0.7 copy-done.5
  3.9 0.0 copy-start.6
  3.9 0.7 copy-done.6
  4.6 0.0 copy-start.3
  4.6 74.2 %exchange.1 = (bf16[128,128,128]{2,1,0:T(8,128)(2,1)S(1)}, s32[8,128]{1,0:T(8,128)S(1)}, bf16[4,512,1024]{2,1,0:T(8,128)(2,1)}) custom-call(s32[3,64]{1,0:T(4,128)S(1)} %bitcast.3, s32[2,64]{1,0:T(2,128)S(1)} %bitcast.4, s32[1]{0:T(128)S(6)} %copy.12.live, s32[64,64]{1,0:T(8,128)S(1)} %copy-done.4, f32[4,64,8,512]{3,2,1,0:T(8,128)} %bitcast.5, ...), custom_call_target="tpu_custom_call" | custom-call | tf_op jit(solution)/shard_map/exchange/pallas_call | solution.py:383
  78.9 0.0 copy-start
  78.9 0.0 copy-done.3
  78.9 4.3 %combine.1.ham = bf16[512,1024]{1,0:T(8,128)(2,1)} custom-call(s32[8,128]{1,0:T(8,128)S(1)} %get-tuple-element.5.info, bf16[128,128,128]{2,1,0:T(8,128)(2,1)S(1)} %get-tuple-element.6.received, bf16[512,1024]{1,0:T(8,128)(2,1)S(1)} %copy-done.3), custom_call_target="tpu_custom_call" | custom-call | tf_op jit(solution)/shard_map/combine/pallas_call | solution.py:467
  83.3 0.0 copy-done
  83.3 0.0 copy-start.1
  83.3 1.2 copy-done.1
  84.5 68.7 %product.1 = f32[512,1024]{1,0:T(8,128)S(1)} custom-call(bf16[512,1024]{1,0:T(8,128)(2,1)S(1)} %copy-done.1, bf16[4,512,1024]{2,1,0:T(8,128)(2,1)S(1)} %copy-done), custom_call_target="tpu_custom_call" | custom-call | tf_op jit(solution)/shard_map/product/pallas_call | solution.py:679
  153.2 1.3 copy.13
Async XLA Ops:
  1.3 1.2 copy-start.2
  2.5 0.8 copy-start.4
  3.3 0.7 copy-start.5
  3.9 0.7 copy-start.6
  4.6 74.3 %copy-start.3 = (bf16[512,1024]{1,0:T(8,128)(2,1)S(1)}, bf16[512,1024]{1,0:T(8,128)(2,1)}, u32[]{:S(2)}) copy-start(bf16[512,1024]{1,0:T(8,128)(2,1)} %core.1) | copy-start | bytes 3145732
  78.9 4.4 %copy-start = (bf16[4,512,1024]{2,1,0:T(8,128)(2,1)S(1)}, bf16[4,512,1024]{2,1,0:T(8,128)(2,1)}, u32[]{:S(2)}) copy-start(bf16[4,512,1024]{2,1,0:T(8,128)(2,1)} %get-tuple-element.7.den) | copy-start | bytes 12582916
  83.3 1.2 copy-start.1

commit v5 on v4

--- a/solution.py
+++ b/solution.py
@@ -21,6 +21,7 @@
 TILE_C = 1024
 HALF = 256
 STRIDE = 51
+PRODUCT_VMEM = 45500000
 MESH = pl.DeviceIdType.MESH
 F32 = jnp.float32
 BF16 = jnp.bfloat16
@@ -422,60 +423,10 @@
     )(offsets, pairs, live, pattern, pot, density, left, right)
 
 
-def combine_kernel(info, received, core, ham, head, after):
-    def clear(b, carry):
-        head[b] = -1
-        return carry
-
-    lax.fori_loop(0, LOCAL, clear, 0)
-
-    def link(s, carry):
-        slot = info[0, s]
-
-        @pl.when(slot >= 0)
-        def _():
-            after[s] = head[slot]
-            head[slot] = s
-
-        return carry
-
-    lax.fori_loop(0, DEVICES, link, 0)
-
-    def more(state):
-        s, total = state
-        return after[s], total + received[s].astype(F32)
-
-    for i in range(ATOM_ROWS):
-        for j in range(ATOM_COLS):
-            block = i * ATOM_COLS + j
-            box = (slice(i * NB, (i + 1) * NB), slice(j * NB, (j + 1) * NB))
-            on = info[1, block] > 0
-
-            @pl.when(on)
-            def _():
-                total = lax.while_loop(
-                    lambda state: state[0] >= 0, more, (head[block], core[box].astype(F32))
-                )[1]
-                ham[box] = total.astype(BF16)
-
-            @pl.when(jnp.logical_not(on))
-            def _():
-                ham[box] = jnp.zeros((NB, NB), BF16)
-
-
-def combine(info, received, core):
-    return pl.pallas_call(
-        combine_kernel,
-        name="combine",
-        out_shape=jax.ShapeDtypeStruct((TILE_R, TILE_C), BF16),
-        in_specs=[smem(), vmem(), vmem()],
-        out_specs=vmem(),
-        scratch_shapes=[pltpu.SMEM((LOCAL,), I32), pltpu.SMEM((DEVICES,), I32)],
-        compiler_params=pltpu.CompilerParams(vmem_limit_bytes=48 << 20),
-    )(info, received, core)
-
-
-def product_kernel(ham, den, out, hbuf, dbuf, load, hsend, dsend, csend, hrecv, drecv):
+def product_kernel(
+    info, received, core_h, den, out, ham,
+    hbuf, dbuf, core_v, sums, table, table_s, load, keep_sem, hsend, dsend, csend, hrecv, drecv,
+):
     row = lax.axis_index("row")
     col = lax.axis_index("col")
     core = row % 2
@@ -532,7 +483,7 @@
     h_up, h_down = col_of(x + 1, 1 - yhi), col_of(x + 3, 1 - yhi)
     d_up, d_down = row_of(1 - ylo, z + 1, core), row_of(1 - ylo, z + 3, core)
 
-    first = [pltpu.make_async_copy(ham, hbuf.at[col], load.at[0])] + [
+    first = [pltpu.make_async_copy(core_h, core_v, load.at[0])] + [
         pltpu.make_async_copy(
             den.at[slot, pl.ds(half * HALF, HALF), :], d_at(r, half), load.at[n + 1]
         )
@@ -548,6 +499,28 @@
         (z_up, col), (z_down, col), (d_partner, col), (other_core, col),
     ):
         pl.semaphore_signal(barrier, inc=1, device_id=peer, device_id_type=MESH)
+    here = lax.broadcasted_iota(I32, (DEVICES, DEVICES), 0)
+    there = lax.broadcasted_iota(I32, (DEVICES, DEVICES), 1)
+    slot_row = jnp.where(info[0:1, :] < 0, LOCAL, info[0:1, :])
+    slot_col = jnp.sum(jnp.where(here == there, slot_row, 0), axis=1, keepdims=True)
+    ahead = jnp.logical_or(
+        slot_row < slot_col, jnp.logical_and(slot_row == slot_col, there < here)
+    )
+    rank = jnp.sum(jnp.where(ahead, 1, 0), axis=1, keepdims=True)
+    ranked = rank == there
+    in_order = jnp.sum(jnp.where(ranked, slot_col, 0), axis=0, keepdims=True)
+    previous = pltpu.roll(jnp.broadcast_to(in_order, (8, DEVICES)), 1, 1)[0:1, :]
+    table[...] = jnp.zeros((8, 128), I32)
+    table[0:1, :] = jnp.sum(jnp.where(ranked, here, 0), axis=0, keepdims=True)
+    table[1:2, :] = jnp.where(
+        jnp.logical_and(in_order == previous, there[0:1, :] > 0), 1, 0
+    )
+    ended = jnp.sum(jnp.where(slot_col <= there, 1, 0), axis=0, keepdims=True)
+    table[2:3, :] = jnp.maximum(ended - 1, 0)
+    table[3:4, :] = jnp.sum(jnp.where(slot_col == there, 1, 0), axis=0, keepdims=True)
+    table[4:5, :] = info[1:2, :]
+    scalars = pltpu.make_async_copy(table, table_s, load.at[6])
+    scalars.start()
     for copy in first:
         copy.wait()
     pl.semaphore_wait(barrier, 7)
@@ -581,10 +554,6 @@
         lax.fori_loop(0, TILE_C // 256, tile, 0)
 
     push("d", d_copy, row, 1, d_partner)
-    for n in range(2):
-        push("h", h_copy, col, n, x_up)
-        push("h", h_copy, col, 1 - n, x_down)
-        push("h", h_copy, col, n, h_partner)
     push("d", d_copy, row, 1, z_up)
     push("d", d_copy, row, 0, z_down)
     push("d", d_copy, d_partner, 0, z_up)
@@ -592,6 +561,30 @@
     push("d", d_copy, z_down, 0, z_up)
     for r, half in ((row, 0), (row, 1), (d_partner, 0), (z_down, 0), (z_up, 1)):
         share(r, half)
+
+    scalars.wait()
+
+    def add(p, total):
+        same = jnp.full((NB, NB), table_s[1, p], I32) > 0
+        total = received[table_s[0, p]].astype(F32) + jnp.where(same, total, 0.0)
+        sums[p] = total
+        return total
+
+    lax.fori_loop(0, DEVICES, add, jnp.zeros((NB, NB), F32))
+    for i in range(ATOM_ROWS):
+        for j in range(ATOM_COLS):
+            block = i * ATOM_COLS + j
+            box = (slice(i * NB, (i + 1) * NB), slice(j * NB, (j + 1) * NB))
+            some = jnp.full((NB, NB), table_s[3, block], I32) > 0
+            on = jnp.full((NB, NB), table_s[4, block], I32) > 0
+            total = core_v[box].astype(F32) + jnp.where(some, sums[table_s[2, block]], 0.0)
+            hbuf[col, i * NB : (i + 1) * NB, j * NB : (j + 1) * NB] = jnp.where(on, total, 0.0).astype(BF16)
+    keep_ham = pltpu.make_async_copy(hbuf.at[col], ham, keep_sem)
+    keep_ham.start()
+    for n in range(2):
+        push("h", h_copy, col, n, x_up)
+        push("h", h_copy, col, 1 - n, x_down)
+        push("h", h_copy, col, n, h_partner)
 
     h_wait(x_down, 0)
     push("h", h_copy, x_down, 0, x_up)
@@ -671,31 +664,35 @@
         multiply(k, False, half)
     d_both(row_of(1 - ylo, z + 2, 1 - core))
     multiply(late, False)
+    keep_ham.wait()
     for copy in sent:
         copy.wait_send()
 
 
-def multiply_all(ham, den):
+def multiply_all(info, received, core, den):
+    dma = pltpu.SemaphoreType.DMA
     return pl.pallas_call(
         product_kernel,
         name="product",
-        out_shape=jax.ShapeDtypeStruct((TILE_R, TILE_C), F32),
-        in_specs=[hbm(), hbm()],
-        out_specs=vmem(),
+        out_shape=(
+            jax.ShapeDtypeStruct((TILE_R, TILE_C), F32),
+            jax.ShapeDtypeStruct((TILE_R, TILE_C), BF16),
+        ),
+        in_specs=[vmem(), vmem(), hbm(), hbm()],
+        out_specs=(vmem(), hbm()),
         scratch_shapes=[
             pltpu.VMEM((COLS, TILE_R, TILE_C), BF16),
             pltpu.VMEM((COLS, 2 * TILE_R, TILE_C), BF16),
-            pltpu.SemaphoreType.DMA((7,)),
-            pltpu.SemaphoreType.DMA((16,)),
-            pltpu.SemaphoreType.DMA((16,)),
-            pltpu.SemaphoreType.DMA((16,)),
-            pltpu.SemaphoreType.DMA((COLS, 2)),
-            pltpu.SemaphoreType.DMA((ROWS, 2)),
+            pltpu.VMEM((TILE_R, TILE_C), BF16),
+            pltpu.VMEM((DEVICES, NB, NB), F32),
+            pltpu.VMEM((8, 128), I32),
+            pltpu.SMEM((8, 128), I32),
+            dma((7,)), dma, dma((16,)), dma((16,)), dma((16,)), dma((COLS, 2)), dma((ROWS, 2)),
         ],
         compiler_params=pltpu.CompilerParams(
-            has_side_effects=True, vmem_limit_bytes=40 << 20, collective_id=1
+            has_side_effects=True, vmem_limit_bytes=PRODUCT_VMEM, collective_id=1
         ),
-    )(ham, den)
+    )(info, received, core, den)
 
 
 def shards(
@@ -705,8 +702,8 @@
         cube_offsets.T, pair_atoms.T, live_count, pattern, potential.reshape(4, 64, 8, 512),
         density, basis_left, basis_right,
     )
-    ham = combine(info, received, core_matrix)
-    return ham, multiply_all(ham, near_den)
+    product, ham = multiply_all(info, received, core_matrix, near_den)
+    return ham, product
 
 
 def solution(mesh):

time: 155 us -> 151 us (0.974)
  Pallas kernels: 147 us -> 144 us
    pallas_call x2 -> x1, Pallas kernels: 73.1 us -> 69.7 us  [multiply_all(): pl.pallas_call(product_kernel, name='product', out_shape=(jax.ShapeDtypeS...]
    unnamed x15 -> x12, local copies, waits for them, and re-layouts: 5.89 us -> 5.63 us
where the time goes in v5:
time: 151 us
  Pallas kernels  144 us (95%)
  local copies, waits for them, and re-layouts  5.63 us (4%)
    pallas_call x1, Pallas kernels, exchange(): pl.pallas_call(exchange_kernel, name='exchange', out_shape=(jax.ShapeDtyp...  74.2 us
    pallas_call x1, Pallas kernels, multiply_all(): pl.pallas_call(product_kernel, name='product', out_shape=(jax.ShapeDtypeS...  69.7 us
    unnamed x12, local copies, waits for them, and re-layouts  5.63 us

profile of v5, /device:TPU:1, one launch (start us, length us, event | category | flops | bytes accessed | tf_op | source)
XLA Modules:
  0.0 150.9 jit_solution(16587508460204464797)
XLA Ops:
  1.3 0.0 copy-start
  1.3 1.2 copy-done
  2.5 0.0 copy-start.2
  2.5 0.8 copy-done.2
  3.3 0.0 copy-start.3
  3.3 0.7 copy-done.3
  3.9 0.0 copy-start.4
  3.9 0.7 copy-done.4
  4.6 0.0 copy-start.1
  4.6 74.2 %exchange.1 = (bf16[128,128,128]{2,1,0:T(8,128)(2,1)S(1)}, s32[8,128]{1,0:T(8,128)S(1)}, bf16[4,512,1024]{2,1,0:T(8,128)(2,1)}) custom-call(s32[3,64]{1,0:T(4,128)S(1)} %bitcast.3, s32[2,64]{1,0:T(2,128)S(1)} %bitcast.4, s32[1]{0:T(128)S(6)} %copy.13.live, s32[64,64]{1,0:T(8,128)S(1)} %copy-done.2, f32[4,64,8,512]{3,2,1,0:T(8,128)} %bitcast.5, ...), custom_call_target="tpu_custom_call" | custom-call | tf_op jit(solution)/shard_map/exchange/pallas_call | solution.py:384
  78.9 0.0 copy-done.1
  78.9 69.7 %product.1 = (f32[512,1024]{1,0:T(8,128)S(1)}, bf16[512,1024]{1,0:T(8,128)(2,1)S(1)}) custom-call(s32[8,128]{1,0:T(8,128)S(1)} %get-tuple-element.7.info, bf16[128,128,128]{2,1,0:T(8,128)(2,1)S(1)} %get-tuple-element.8.received, bf16[512,1024]{1,0:T(8,128)(2,1)S(1)} %copy-done.1, bf16[4,512,1024]{2,1,0:T(8,128)(2,1)} %get-tuple-element.9.den), custom_call_target="tpu_custom_call" | custom-call | tf_op jit(solution)/shard_map/product/pallas_call | solution.py:674
  148.6 1.0 copy.14
  149.6 1.3 copy.15
Async XLA Ops:
  1.3 1.2 copy-start
  2.5 0.8 copy-start.2
  3.3 0.7 copy-start.3
  3.9 0.7 copy-start.4
  4.6 74.3 %copy-start.1 = (bf16[512,1024]{1,0:T(8,128)(2,1)S(1)}, bf16[512,1024]{1,0:T(8,128)(2,1)}, u32[]{:S(2)}) copy-start(bf16[512,1024]{1,0:T(8,128)(2,1)} %core_h.1) | copy-start | bytes 3145732

commit v6 on v5

--- a/solution.py
+++ b/solution.py
@@ -543,7 +543,7 @@
             lines = pl.ds(pl.multiple_of(half * HALF, HALF), HALF)
 
         def tile(n, carry):
-            columns = pl.ds(pl.multiple_of(n * 256, 256), 256)
+            columns = pl.ds(pl.multiple_of(n * 512, 512), 512)
             part = jnp.dot(hbuf[k, lines], dbuf[k, :, columns], preferred_element_type=F32)
             if start:
                 out[lines, columns] = part
@@ -551,7 +551,7 @@
                 out[lines, columns] += part
             return carry
 
-        lax.fori_loop(0, TILE_C // 256, tile, 0)
+        lax.fori_loop(0, TILE_C // 512, tile, 0)
 
     push("d", d_copy, row, 1, d_partner)
     push("d", d_copy, row, 1, z_up)
@@ -570,7 +570,7 @@
         sums[p] = total
         return total
 
-    lax.fori_loop(0, DEVICES, add, jnp.zeros((NB, NB), F32))
+    lax.fori_loop(0, DEVICES, add, jnp.zeros((NB, NB), F32), unroll=4)
     for i in range(ATOM_ROWS):
         for j in range(ATOM_COLS):
             block = i * ATOM_COLS + j

time: 151 us -> 149 us (0.987)
  Pallas kernels: 144 us -> 141 us
    pallas_call x1, Pallas kernels: 69.7 us -> 67.1 us  [multiply_all(): pl.pallas_call(product_kernel, name='product', out_shape=(jax.ShapeDtypeS...]
where the time goes in v6:
time: 149 us; the launch traced here: 148 us
  Pallas kernels  141 us (95%)
  local copies, waits for them, and re-layouts  5.63 us (4%)
    pallas_call x1, Pallas kernels, exchange(): pl.pallas_call(exchange_kernel, name='exchange', out_shape=(jax.ShapeDtyp...  74.2 us
    pallas_call x1, Pallas kernels, multiply_all(): pl.pallas_call(product_kernel, name='product', out_shape=(jax.ShapeDtypeS...  67.1 us
    unnamed x12, local copies, waits for them, and re-layouts  5.63 us

profile of v6, /device:TPU:1, one launch (start us, length us, event | category | flops | bytes accessed | tf_op | source)
XLA Modules:
  0.0 148.3 jit_solution(13381524508001962271)
XLA Ops:
  1.3 0.0 copy-start
  1.3 1.2 copy-done
  2.5 0.0 copy-start.2
  2.5 0.8 copy-done.2
  3.3 0.0 copy-start.3
  3.3 0.7 copy-done.3
  3.9 0.0 copy-start.4
  3.9 0.7 copy-done.4
  4.6 0.0 copy-start.1
  4.6 74.2 %exchange.1 = (bf16[128,128,128]{2,1,0:T(8,128)(2,1)S(1)}, s32[8,128]{1,0:T(8,128)S(1)}, bf16[4,512,1024]{2,1,0:T(8,128)(2,1)}) custom-call(s32[3,64]{1,0:T(4,128)S(1)} %bitcast.3, s32[2,64]{1,0:T(2,128)S(1)} %bitcast.4, s32[1]{0:T(128)S(6)} %copy.13.live, s32[64,64]{1,0:T(8,128)S(1)} %copy-done.2, f32[4,64,8,512]{3,2,1,0:T(8,128)} %bitcast.5, ...), custom_call_target="tpu_custom_call" | custom-call | tf_op jit(solution)/shard_map/exchange/pallas_call | solution.py:384
  78.9 0.0 copy-done.1
  78.9 67.1 %product.1 = (f32[512,1024]{1,0:T(8,128)S(1)}, bf16[512,1024]{1,0:T(8,128)(2,1)S(1)}) custom-call(s32[8,128]{1,0:T(8,128)S(1)} %get-tuple-element.7.info, bf16[128,128,128]{2,1,0:T(8,128)(2,1)S(1)} %get-tuple-element.8.received, bf16[512,1024]{1,0:T(8,128)(2,1)S(1)} %copy-done.1, bf16[4,512,1024]{2,1,0:T(8,128)(2,1)} %get-tuple-element.9.den), custom_call_target="tpu_custom_call" | custom-call | tf_op jit(solution)/shard_map/product/pallas_call | solution.py:674
  146.0 1.0 copy.14
  147.0 1.3 copy.15
Async XLA Ops:
  1.3 1.2 copy-start
  2.5 0.8 copy-start.2
  3.3 0.7 copy-start.3
  3.9 0.7 copy-start.4
  4.6 74.3 %copy-start.1 = (bf16[512,1024]{1,0:T(8,128)(2,1)S(1)}, bf16[512,1024]{1,0:T(8,128)(2,1)}, u32[]{:S(2)}) copy-start(bf16[512,1024]{1,0:T(8,128)(2,1)} %core_h.1) | copy-start | bytes 3145732

commit v7 on v6

--- a/solution.py
+++ b/solution.py
@@ -76,7 +76,7 @@
         pltpu.make_async_copy(a, b, small_sem.at[n])
         for n, (a, b) in enumerate(((offsets_h, offsets), (pairs_h, pairs), (pattern_h, pattern)))
     ]
-    for copy in small + loads[:1] + pot_loads + loads[1:]:
+    for copy in small:
         copy.start()
     barrier = pltpu.get_barrier_semaphore()
 
@@ -96,6 +96,8 @@
     lax.fori_loop(1, COLS, greet_row, 0)
     lax.fori_loop(1, ROWS, greet_col, 0)
 
+    for copy in loads[:1] + pot_loads + loads[1:]:
+        copy.start()
     for copy in small:
         copy.wait()
     own_off[...] = jnp.zeros((8, 128), I32)
@@ -285,7 +287,7 @@
         return made
 
     for copy in off_copies:
-        copy.wait()
+        copy.wait_recv()
     other_scalars = [
         pltpu.make_async_copy(other_off.at[n], off_s.at[n + 1], copy_sem.at[n + 2]) for n in range(2)
     ]
@@ -327,7 +329,7 @@
     own_id = pltpu.make_async_copy(ids.at[me], received_ids.at[me], local.at[0])
     own_id.start()
     for copy in near:
-        copy.wait()
+        copy.wait_recv()
     whole = jnp.concatenate(
         [low[...].astype(F32), own_piece[0], own_piece[1], high[...].astype(F32)], axis=1
     )
@@ -364,6 +366,8 @@
     own_block.start()
     own_id.wait()
     keep_den.wait()
+    for copy in near + off_copies:
+        copy.wait_send()
     own_block.wait()
     all_but_one = pl.ds(0, DEVICES - 1)
     ids_done = pltpu.make_async_remote_copy(
@@ -543,7 +547,7 @@
             lines = pl.ds(pl.multiple_of(half * HALF, HALF), HALF)
 
         def tile(n, carry):
-            columns = pl.ds(pl.multiple_of(n * 512, 512), 512)
+            columns = pl.ds(pl.multiple_of(n * 1024, 1024), 1024)
             part = jnp.dot(hbuf[k, lines], dbuf[k, :, columns], preferred_element_type=F32)
             if start:
                 out[lines, columns] = part
@@ -551,7 +555,7 @@
                 out[lines, columns] += part
             return carry
 
-        lax.fori_loop(0, TILE_C // 512, tile, 0)
+        lax.fori_loop(0, TILE_C // 1024, tile, 0)
 
     push("d", d_copy, row, 1, d_partner)
     push("d", d_copy, row, 1, z_up)

time: 149 us -> 148 us (level)
  no operation moved by 1% of the time
where the time goes in v7:
time: 148 us
  Pallas kernels  141 us (95%)
  local copies, waits for them, and re-layouts  5.63 us (4%)
    pallas_call x1, Pallas kernels, exchange(): pl.pallas_call(exchange_kernel, name='exchange', out_shape=(jax.ShapeDtyp...  74.2 us
    pallas_call x1, Pallas kernels, multiply_all(): pl.pallas_call(product_kernel, name='product', out_shape=(jax.ShapeDtypeS...  66.8 us
    unnamed x12, local copies, waits for them, and re-layouts  5.63 us

profile of v7, /device:TPU:1, one launch (start us, length us, event | category | flops | bytes accessed | tf_op | source)
XLA Modules:
  0.0 147.9 jit_solution(833926077503982355)
XLA Ops:
  1.3 0.0 copy-start
  1.3 1.2 copy-done
  2.5 0.0 copy-start.2
  2.5 0.8 copy-done.2
  3.3 0.0 copy-start.3
  3.3 0.7 copy-done.3
  3.9 0.0 copy-start.4
  3.9 0.7 copy-done.4
  4.6 0.0 copy-start.1
  4.6 74.2 %exchange.1 = (bf16[128,128,128]{2,1,0:T(8,128)(2,1)S(1)}, s32[8,128]{1,0:T(8,128)S(1)}, bf16[4,512,1024]{2,1,0:T(8,128)(2,1)}) custom-call(s32[3,64]{1,0:T(4,128)S(1)} %bitcast.3, s32[2,64]{1,0:T(2,128)S(1)} %bitcast.4, s32[1]{0:T(128)S(6)} %copy.13.live, s32[64,64]{1,0:T(8,128)S(1)} %copy-done.2, f32[4,64,8,512]{3,2,1,0:T(8,128)} %bitcast.5, ...), custom_call_target="tpu_custom_call" | custom-call | tf_op jit(solution)/shard_map/exchange/pallas_call | solution.py:388
  78.8 0.0 copy-done.1
  78.8 66.8 %product.1 = (f32[512,1024]{1,0:T(8,128)S(1)}, bf16[512,1024]{1,0:T(8,128)(2,1)S(1)}) custom-call(s32[8,128]{1,0:T(8,128)S(1)} %get-tuple-element.7.info, bf16[128,128,128]{2,1,0:T(8,128)(2,1)S(1)} %get-tuple-element.8.received, bf16[512,1024]{1,0:T(8,128)(2,1)S(1)} %copy-done.1, bf16[4,512,1024]{2,1,0:T(8,128)(2,1)} %get-tuple-element.9.den), custom_call_target="tpu_custom_call" | custom-call | tf_op jit(solution)/shard_map/product/pallas_call | solution.py:678
  145.6 1.0 copy.14
  146.6 1.3 copy.15
Async XLA Ops:
  1.3 1.2 copy-start
  2.5 0.8 copy-start.2
  3.3 0.7 copy-start.3
  3.9 0.7 copy-start.4
  4.6 74.2 %copy-start.1 = (bf16[512,1024]{1,0:T(8,128)(2,1)S(1)}, bf16[512,1024]{1,0:T(8,128)(2,1)}, u32[]{:S(2)}) copy-start(bf16[512,1024]{1,0:T(8,128)(2,1)} %core_h.1) | copy-start | bytes 3145732
